TPU v7x, 256 devices: a whole 4x4x8 slice. The times are simulated.
256 devices in a mesh: seq: 32 (over z, y), head: 8 (over x, core).
Axes of the slice: x: 4, y: 4, z: 8, core: 2. Of those that a mesh axis runs over, the one named last changes fastest.
Arguments:
- queries: bfloat16 [16384, 64, 128], P(('seq', 'head')), may hold values from -6 to 6
- key_heads: bfloat16 [16384, 64, 128], P(('seq', 'head')), may hold values from -6 to 6
- value_heads: bfloat16 [16384, 64, 128], P(('seq', 'head')), may hold values from -6 to 6
- grad_output: bfloat16 [16384, 64, 128], P(('seq', 'head')), may hold values from -6 to 6
- doc_lengths: int32 [16], replicated, may hold values from 1 to 8192, 16384 in all
Outputs:
- query_gradient: bfloat16 [16384, 64, 128], P(('seq', 'head'))
- lookup_derivative: bfloat16 [16384, 64, 128], P(('seq', 'head'))
- content_derivative: bfloat16 [16384, 64, 128], P(('seq', 'head'))
Inputs may be any that keep to these rules, and one draw needn't show every extreme that they name: `doc_lengths`: the lengths sum to 16384; the longest is exactly 8192.
All inputs are finite; a program needn't handle non-finite values.
Results may differ from a plain program's by a relative error of at most 0.005.
Values may be sent and summed in bfloat16 or wider, within the bound.
A program may use at most 128 MiB of HBM per device.

v0:
```python
import math

import jax
import jax.numpy as jnp
from jax import lax
from jax.sharding import PartitionSpec as P

BLOCK = 256


def entering(value, axis, combine, identity, reverse):
    count, place = (lax.axis_size(axis), lax.axis_index(axis))
    everything = jax.tree.map(lambda part: lax.all_gather(part, axis), value)
    start = jax.tree.map(
        lambda part, zero: jnp.broadcast_to(jnp.asarray(zero, part.dtype), part.shape),
        value,
        identity,
    )

    def step(k, before):
        at = count - 1 - k if reverse else k
        reached = at > place if reverse else at < place
        new = combine(before, jax.tree.map(lambda part: part[at], everything))
        return jax.tree.map(lambda a, b: jnp.where(reached, a, b), new, before)

    return lax.fori_loop(0, count, step, start)


def doc_index(doc_lengths, positions):
    ends = jnp.cumsum(doc_lengths)
    return jnp.sum((ends[None, :] <= positions[:, None]).astype(jnp.int32), axis=1)


def masked_state(left_rows, rightward_rows, selected):
    weighted_values = left_rows * selected.astype(jnp.bfloat16)[:, None, None]
    return jnp.einsum(
        "rfb,rfc->fbc", weighted_values, rightward_rows, preferred_element_type=jnp.float32
    )


def combine_states(earlier, later):
    return (later[0] + (1.0 - later[1]) * earlier[0], jnp.maximum(earlier[1], later[1]))


def local(queries, key_heads, value_heads, grad_output, doc_lengths):
    query_rows, key_rows, value_rows, grad_rows = (
        lax.all_to_all(queries, "head", split_axis=1, concat_axis=0, tiled=True),
        lax.all_to_all(key_heads, "head", split_axis=1, concat_axis=0, tiled=True),
        lax.all_to_all(value_heads, "head", split_axis=1, concat_axis=0, tiled=True),
        lax.all_to_all(grad_output, "head", split_axis=1, concat_axis=0, tiled=True),
    )
    tok_local, head_count, head_width = query_rows.shape
    tokens_all = tok_local * lax.axis_size("seq")
    scaling = 1.0 / math.sqrt(head_width * (tokens_all // 2))
    my_index = lax.axis_index("seq")
    row_start = my_index * tok_local
    row_ids = jnp.arange(tok_local, dtype=jnp.int32)
    doc_of = doc_index(doc_lengths, row_start + row_ids)
    edge_docs = doc_index(doc_lengths, jnp.stack([row_start - 1, row_start + tok_local]))
    doc_before = edge_docs[0]
    doc_after = edge_docs[1]
    zero_state = jnp.zeros((head_count, head_width, head_width), jnp.float32)
    block_count = tok_local // BLOCK
    first_docs = [doc_of[b * BLOCK] for b in range(block_count)]
    last_docs = [doc_of[(b + 1) * BLOCK - 1] for b in range(block_count)]
    tail_pieces = []
    head_pieces = []
    for block_id in range(block_count):
        low_row = block_id * BLOCK
        high_row = low_row + BLOCK
        block_docs = doc_of[low_row:high_row]
        tail_pieces.append(
            masked_state(
                key_rows[low_row:high_row],
                value_rows[low_row:high_row],
                block_docs == last_docs[block_id],
            )
        )
        head_pieces.append(
            masked_state(
                query_rows[low_row:high_row],
                grad_rows[low_row:high_row],
                block_docs == first_docs[block_id],
            )
        )
    local_a = []
    running = zero_state
    prev_last = jnp.int32(-1)
    for block_id in range(block_count):
        local_a.append(jnp.where(first_docs[block_id] == prev_last, running, jnp.float32(0.0)))
        running = (
            jnp.where(last_docs[block_id] == prev_last, running, jnp.float32(0.0))
            + tail_pieces[block_id]
        )
        prev_last = last_docs[block_id]
    a_sum = running
    local_b = [zero_state] * block_count
    running = zero_state
    next_first = jnp.int32(-1)
    for block_id in reversed(range(block_count)):
        local_b[block_id] = jnp.where(last_docs[block_id] == next_first, running, jnp.float32(0.0))
        running = (
            jnp.where(first_docs[block_id] == next_first, running, jnp.float32(0.0))
            + head_pieces[block_id]
        )
        next_first = first_docs[block_id]
    a_flag = (doc_before != doc_of[-1]).astype(jnp.float32)
    incoming_a, _ = entering(
        (a_sum, a_flag), "seq", combine_states, (zero_state, jnp.float32(0.0)), False
    )
    b_flag = (doc_of[0] != doc_after).astype(jnp.float32)
    incoming_b, _ = entering(
        (running, b_flag), "seq", combine_states, (zero_state, jnp.float32(0.0)), True
    )
    local_ids = jnp.arange(BLOCK, dtype=jnp.int32)
    causal = local_ids[:, None] >= local_ids[None, :]
    query_parts, key_parts, value_parts = ([], [], [])
    for block_id in range(block_count):
        low_row = block_id * BLOCK
        high_row = low_row + BLOCK
        block_docs = doc_of[low_row:high_row]
        first_doc = first_docs[block_id]
        last_doc = last_docs[block_id]
        first_state = local_a[block_id] + incoming_a * (first_doc == doc_before).astype(jnp.float32)
        other_memory = local_b[block_id] + incoming_b * (last_doc == doc_after).astype(jnp.float32)
        first_state = lax.optimization_barrier((scaling * first_state).astype(jnp.bfloat16))
        other_memory = lax.optimization_barrier((scaling * other_memory).astype(jnp.bfloat16))
        probe_tile = query_rows[low_row:high_row]
        block_of_keys = key_rows[low_row:high_row]
        value_block = value_rows[low_row:high_row]
        tile_derivative = grad_rows[low_row:high_row]
        same_doc = ((block_docs[:, None] == block_docs[None, :]) & causal).astype(jnp.float32)
        affinity_derivative = (
            jnp.einsum(
                "thd,shd->hts", tile_derivative, value_block, preferred_element_type=jnp.float32
            )
            * scaling
            * same_doc[None]
        )
        affinity_derivative = lax.optimization_barrier(affinity_derivative.astype(jnp.bfloat16))
        affinity_table = (
            jnp.einsum(
                "thd,shd->hts", probe_tile, block_of_keys, preferred_element_type=jnp.float32
            )
            * scaling
            * same_doc[None]
        )
        affinity_table = lax.optimization_barrier(affinity_table.astype(jnp.bfloat16))
        leading_head_rows = (block_docs == first_doc).astype(jnp.bfloat16)[:, None, None]
        remaining_lines = (block_docs == last_doc).astype(jnp.bfloat16)[:, None, None]
        query_gradient = jnp.einsum(
            "lca,alg->clg", affinity_derivative, block_of_keys, preferred_element_type=jnp.float32
        )
        query_gradient = query_gradient + jnp.einsum(
            "dgj,gsj->dgs",
            tile_derivative * leading_head_rows,
            first_state,
            preferred_element_type=jnp.float32,
        )
        lookup_derivative = jnp.einsum(
            "gjh,jgt->hgt", affinity_derivative, probe_tile, preferred_element_type=jnp.float32
        )
        lookup_derivative = lookup_derivative + jnp.einsum(
            "lcg,cng->lcn",
            value_block * remaining_lines,
            other_memory,
            preferred_element_type=jnp.float32,
        )
        content_derivative = jnp.einsum(
            "gjh,jgt->hgt", affinity_table, tile_derivative, preferred_element_type=jnp.float32
        )
        content_derivative = content_derivative + jnp.einsum(
            "qpf,pfe->qpe",
            block_of_keys * remaining_lines,
            other_memory,
            preferred_element_type=jnp.float32,
        )
        query_parts.append(query_gradient.astype(jnp.bfloat16))
        key_parts.append(lookup_derivative.astype(jnp.bfloat16))
        value_parts.append(content_derivative.astype(jnp.bfloat16))
    query_gradient = jnp.concatenate(query_parts, axis=0)
    lookup_derivative = jnp.concatenate(key_parts, axis=0)
    content_derivative = jnp.concatenate(value_parts, axis=0)
    return (
        lax.all_to_all(query_gradient, "head", split_axis=0, concat_axis=1, tiled=True),
        lax.all_to_all(lookup_derivative, "head", split_axis=0, concat_axis=1, tiled=True),
        lax.all_to_all(content_derivative, "head", split_axis=0, concat_axis=1, tiled=True),
    )


def solution(mesh):
    placed = (
        P(("seq", "head"), None, None),
        P(("seq", "head"), None, None),
        P(("seq", "head"), None, None),
        P(("seq", "head"), None, None),
        P(),
    )
    return jax.shard_map(
        local,
        mesh=mesh,
        in_specs=placed,
        out_specs=(
            P(("seq", "head"), None, None),
            P(("seq", "head"), None, None),
            P(("seq", "head"), None, None),
        ),
        check_vma=False,
    )
```

profile of v0, /device:TPU:1, one launch (start us, length us, event | category | flops | bytes accessed | tf_op | source)
XLA Modules:
  0.0 478.1 jit_solution(14347616097846203733)
XLA Ops:
  7.2 3.0 copy.87
  10.1 6.7 %all-to-all-start = ((bf16[64,64,128]{2,0,1:T(8,128)(2,1)}), bf16[64,64,128]{2,0,1:T(8,128)(2,1)S(1)}, u32[]{:S(2)}, u32[]{:S(2)}) async-start(bf16[64,64,128]{2,0,1:T(8,128)(2,1)} %copy.87), calls=%async_computation | async-start | bytes 2097152 | tf_op jit(solution)/shard_map/all_to_all | solution.py:50
  18.5 13.3 %all-to-all-done = bf16[64,64,128]{2,0,1:T(8,128)(2,1)S(1)} async-done(((bf16[64,64,128]{2,0,1:T(8,128)(2,1)}), bf16[64,64,128]{2,0,1:T(8,128)(2,1)S(1)}, u32[]{:S(2)}, u32[]{:S(2)}) %all-to-all-start) | async-done | bytes 1048608 | tf_op jit(solution)/shard_map/all_to_all | solution.py:50
  31.8 4.4 all-to-all-start.4
  38.5 2.4 compare_convert_fusion.1
  41.1 10.1 %all-to-all-done.4 = bf16[64,64,128]{2,0,1:T(8,128)(2,1)S(1)} async-done(((bf16[64,64,128]{2,0,1:T(8,128)(2,1)}), bf16[64,64,128]{2,0,1:T(8,128)(2,1)S(1)}, u32[]{:S(2)}, u32[]{:S(2)}) %all-to-all-start.4) | async-done | bytes 1048608 | tf_op jit(solution)/shard_map/all_to_all | solution.py:47
  55.6 4.6 all-to-all-start.2
  61.8 13.3 %all-to-all-done.2 = bf16[64,64,128]{2,0,1:T(8,128)(2,1)S(1)} async-done(((bf16[64,64,128]{2,0,1:T(8,128)(2,1)}), bf16[64,64,128]{2,0,1:T(8,128)(2,1)S(1)}, u32[]{:S(2)}, u32[]{:S(2)}) %all-to-all-start.2) | async-done | bytes 1048608 | tf_op jit(solution)/shard_map/all_to_all | solution.py:48
  75.2 4.4 all-to-all-start.1
  81.9 12.7 %all-to-all-done.1 = bf16[64,64,128]{2,0,1:T(8,128)(2,1)S(1)} async-done(((bf16[64,64,128]{2,0,1:T(8,128)(2,1)}), bf16[64,64,128]{2,0,1:T(8,128)(2,1)S(1)}, u32[]{:S(2)}, u32[]{:S(2)}) %all-to-all-start.1) | async-done | bytes 1048608 | tf_op jit(solution)/shard_map/all_to_all | solution.py:49
  112.4 66.1 %all-reduce.2 = (f32[32]{0:T(128)S(1)}, f32[32]{0:T(128)S(1)}) all-reduce(f32[32]{0:T(128)S(1)} %dynamic-update-slice, f32[32]{0:T(128)S(1)} %dynamic-update-slice.1), channel_id=1, replica_groups=mesh['seq'=32,'head'=8] {'seq'}, use_global_device_ids=true, to_apply=%add | all-reduce | flops 64 | bytes 512
  190.5 4.4 all-gather.7.cloned.1.call-done
  194.9 84.4 %while.31 = (s32[]{:T(128)}, f32[8,128,128]{2,1,0:T(8,128)S(1)}, s32[]{:T(128)}, f32[32,8,128,128]{3,2,1,0:T(8,128)}, f32[32]{0:T(128)S(1)}, /*index=5*/s32[]{:T(128)}, s32[]{:T(128)}, s32[]{:T(128)}, s32[]{:T(128)}, f32[1]{0:T(128)}) while((s32[]{:T(128)}, f32[8,128,128]{2,1,0:T(8,128)S(1)}, s32[]{:T(128)}, ...), condition=%wide.region_6.7_spmd.clone, body=%wide.region_5.6_spmd.clone.sunk | while | flops 524297 | bytes 1573063 | solution.py:26
  280.7 1.7 fusion.12
  282.9 1.7 copy.116
  284.5 14.3 %all-to-all-start.6 = ((bf16[512,8,128]{2,1,0:T(8,128)(2,1)}), bf16[512,8,128]{2,1,0:T(8,128)(2,1)}, u32[]{:S(2)}, u32[]{:S(2)}) async-start(bf16[512,8,128]{2,1,0:T(8,128)(2,1)} %copy.116), calls=%async_computation.6 | async-start | bytes 2097152 | tf_op jit(solution)/shard_map/all_to_all | solution.py:187
  298.9 35.7 %all-gather.5.cloned.1.call-done = f32[256,128,128]{2,1,0:T(8,128)} async-done(((f32[8,128,128]{2,1,0:T(8,128)}), f32[256,128,128]{2,1,0:T(8,128)}) %all-gather.5.cloned.1.call-update) | async-done | bytes 16777232 | tf_op jit(solution)/shard_map/all_gather | solution.py:13
  334.6 91.5 %while.30 = (s32[]{:T(128)}, f32[8,128,128]{2,1,0:T(8,128)S(1)}, s32[]{:T(128)}, f32[32,8,128,128]{3,2,1,0:T(8,128)}, f32[32]{0:T(128)S(1)}, /*index=5*/s32[]{:T(128)}, f32[1]{0:T(128)}, s32[]{:T(128)}) while((s32[]{:T(128)}, f32[8,128,128]{2,1,0:T(8,128)S(1)}, s32[]{:T(128)}, f32[32,8,128,128]{3,2,1,0:T(8,128)}, f32[32]{0:T(128)S(1)}, ...), condition=%wide.region_4.5_spmd.clone, body=%wide.region_3.4_spmd.clone.sunk | while | flops 524293 | bytes 1573001 | solution.py:26
  429.7 5.8 %all-to-all-start.5 = ((bf16[512,8,128]{2,1,0:T(8,128)(2,1)}), bf16[512,8,128]{2,1,0:T(8,128)(2,1)}, u32[]{:S(2)}, u32[]{:S(2)}) async-start(bf16[512,8,128]{2,1,0:T(8,128)(2,1)} %copy.108), calls=%async_computation.5 | async-start | bytes 2097152 | tf_op jit(solution)/shard_map/all_to_all | solution.py:186
  438.8 11.8 %all-to-all-done.5 = bf16[512,8,128]{2,1,0:T(8,128)(2,1)} async-done(((bf16[512,8,128]{2,1,0:T(8,128)(2,1)}), bf16[512,8,128]{2,1,0:T(8,128)(2,1)}, u32[]{:S(2)}, u32[]{:S(2)}) %all-to-all-start.5) | async-done | bytes 1048608 | tf_op jit(solution)/shard_map/all_to_all | solution.py:186
  450.6 4.4 all-to-all-start.3
  455.0 2.5 copy.141
  457.5 2.5 copy.142
  460.0 10.0 %all-to-all-done.3 = bf16[512,8,128]{2,1,0:T(8,128)(2,1)S(1)} async-done(((bf16[512,8,128]{2,1,0:T(8,128)(2,1)}), bf16[512,8,128]{2,1,0:T(8,128)(2,1)S(1)}, u32[]{:S(2)}, u32[]{:S(2)}) %all-to-all-start.3) | async-done | bytes 1048608 | tf_op jit(solution)/shard_map/all_to_all | solution.py:185
  (239 shorter events, 173.3 us)
Async XLA Ops:
  7.2 9.6 %copy-start.20 = (bf16[64,64,128]{2,1,0:T(8,128)(2,1)S(1)}, bf16[64,64,128]{2,1,0:T(8,128)(2,1)}, u32[]{:S(2)}) copy-start(bf16[64,64,128]{2,1,0:T(8,128)(2,1)} %param.9) | copy-start | bytes 3145732
  10.1 21.7 %all-to-all-start = ((bf16[64,64,128]{2,0,1:T(8,128)(2,1)}), bf16[64,64,128]{2,0,1:T(8,128)(2,1)S(1)}, u32[]{:S(2)}, u32[]{:S(2)}) async-start(bf16[64,64,128]{2,0,1:T(8,128)(2,1)} %copy.87), calls=%async_computation | async-start | bytes 2097152 | tf_op jit(solution)/shard_map/all_to_all | solution.py:50
  16.8 19.4 %copy-start.23 = (s32[16]{0:T(128)S(1)}, s32[16]{0:T(128)}, u32[]{:S(2)}) copy-start(s32[16]{0:T(128)} %param.13) | copy-start | bytes 196
  31.8 19.4 %all-to-all-start.4 = ((bf16[64,64,128]{2,0,1:T(8,128)(2,1)}), bf16[64,64,128]{2,0,1:T(8,128)(2,1)S(1)}, u32[]{:S(2)}, u32[]{:S(2)}) async-start(bf16[64,64,128]{2,0,1:T(8,128)(2,1)} %copy.100), calls=%async_computation.4 | async-start | bytes 2097152 | tf_op jit(solution)/shard_map/all_to_all | solution.py:47
  36.2 158.7 %all-gather.7.cloned.1.call-start = ((), (), s32[]{:S(2)}) async-start(), calls=%async_computation.8 | async-start | bytes 17301504 | tf_op jit(solution)/shard_map/all_gather | solution.py:13
  51.4 2.5 copy-start.3
  51.4 2.5 copy-start.21
  55.6 4.6 copy-start.22
  55.6 19.6 %all-to-all-start.2 = ((bf16[64,64,128]{2,0,1:T(8,128)(2,1)}), bf16[64,64,128]{2,0,1:T(8,128)(2,1)S(1)}, u32[]{:S(2)}, u32[]{:S(2)}) async-start(bf16[64,64,128]{2,0,1:T(8,128)(2,1)} %copy.92), calls=%async_computation.2 | async-start | bytes 2097152 | tf_op jit(solution)/shard_map/all_to_all | solution.py:48
  75.2 19.4 %all-to-all-start.1 = ((bf16[64,64,128]{2,0,1:T(8,128)(2,1)}), bf16[64,64,128]{2,0,1:T(8,128)(2,1)S(1)}, u32[]{:S(2)}, u32[]{:S(2)}) async-start(bf16[64,64,128]{2,0,1:T(8,128)(2,1)} %copy.89), calls=%async_computation.1 | async-start | bytes 2097152 | tf_op jit(solution)/shard_map/all_to_all | solution.py:49
  79.6 255.0 %all-gather.5.cloned.1.call-start = ((), (), s32[]{:S(2)}) async-start(), calls=%async_computation.7 | async-start | bytes 17301504 | tf_op jit(solution)/shard_map/all_gather | solution.py:13
  96.9 13.4 %copy-start.24 = (u32[256]{0:T(256)S(1)}, u32[256]{0:T(256)}, u32[]{:S(2)}) copy-start(u32[256]{0:T(256)} %constant.113) | copy-start | bytes 3076
  178.5 1.7 copy-start.4
  178.6 2.0 copy-start.1
  279.4 3.0 copy-start.17
  280.7 1.7 copy-start.19
  284.5 145.2 %all-to-all-start.6 = ((bf16[512,8,128]{2,1,0:T(8,128)(2,1)}), bf16[512,8,128]{2,1,0:T(8,128)(2,1)}, u32[]{:S(2)}, u32[]{:S(2)}) async-start(bf16[512,8,128]{2,1,0:T(8,128)(2,1)} %copy.116), calls=%async_computation.6 | async-start | bytes 2097152 | tf_op jit(solution)/shard_map/all_to_all | solution.py:187
  334.6 91.5 %copy-start.2 = (bf16[4,64,8,128]{3,1,0,2:T(8,128)(2,1)S(1)}, bf16[4,64,8,128]{3,1,0,2:T(8,128)(2,1)}, u32[]{:S(2)}) copy-start(bf16[4,64,8,128]{3,1,0,2:T(8,128)(2,1)} %copy-done) | copy-start | bytes 1572868
  334.6 91.5 %copy-start.16 = (f32[256,8,128]{2,0,1:T(8,128)S(1)}, f32[256,8,128]{2,0,1:T(8,128)}, u32[]{:S(2)}) copy-start(f32[256,8,128]{2,0,1:T(8,128)} %convolution_bitcast_fusion.9) | copy-start | bytes 3145732
  426.1 1.5 copy-start.15
  428.0 7.5 %copy-start.11 = (f32[8,128,128]{2,1,0:T(8,128)S(1)}, f32[8,128,128]{2,1,0:T(8,128)}, u32[]{:S(2)}) copy-start(f32[8,128,128]{2,1,0:T(8,128)} %copy-done.10) | copy-start | bytes 1572868
  429.7 6.0 %copy-start.14 = (f32[256,8,128]{2,0,1:T(8,128)S(1)}, f32[256,8,128]{2,0,1:T(8,128)}, u32[]{:S(2)}) copy-start(f32[256,8,128]{2,0,1:T(8,128)} %convolution_bitcast_fusion.11) | copy-start | bytes 3145732
  429.7 20.9 %all-to-all-start.5 = ((bf16[512,8,128]{2,1,0:T(8,128)(2,1)}), bf16[512,8,128]{2,1,0:T(8,128)(2,1)}, u32[]{:S(2)}, u32[]{:S(2)}) async-start(bf16[512,8,128]{2,1,0:T(8,128)(2,1)} %copy.108), calls=%async_computation.5 | async-start | bytes 2097152 | tf_op jit(solution)/shard_map/all_to_all | solution.py:186
  450.6 19.4 %all-to-all-start.3 = ((bf16[512,8,128]{2,1,0:T(8,128)(2,1)}), bf16[512,8,128]{2,1,0:T(8,128)(2,1)S(1)}, u32[]{:S(2)}, u32[]{:S(2)}) async-start(bf16[512,8,128]{2,1,0:T(8,128)(2,1)} %copy.98), calls=%async_computation.3 | async-start | bytes 2097152 | tf_op jit(solution)/shard_map/all_to_all | solution.py:185
  (10 other events, 10.6 us)
Sparse Core Ops, SparseCore 0:
  54.1 140.8 all-gather.6
  197.5 136.9 all-gather.4
where the time goes:
time: 483 us; the launch traced here: 478 us
  waiting for transfers between devices  111 us (23%)
  other arithmetic  99.8 us (21%)
  local copies, waits for them, and re-layouts  67.9 us (14%)
  blocking collectives  66.1 us (14%)
  starting transfers between devices  44.6 us (9%)
  loops' own time  41.8 us (9%)
  between operations  27.1 us (6%)
  matrix products  19.4 us (4%)
    select_n x64, other arithmetic, step(): return jax.tree.map(lambda a, b: jnp.where(reached, a, b), new, before)  95.1 us
    unnamed x1, blocking collectives  66.1 us
    another operation x2, loops' own time, entering(): return lax.fori_loop(0, count, step, start)  41.8 us
    all_gather x2, waiting for transfers between devices, entering(): everything = jax.tree.map(lambda part: lax.all_gather(part, axis), value)  40.1 us
    dynamic_slice x64, local copies, waits for them, and re-layouts, step(): new = combine(before, jax.tree.map(lambda part: part[at], everything))  39.1 us
    unnamed x59, local copies, waits for them, and re-layouts  14.5 us
    all_to_all x1, starting transfers between devices, local(): lax.all_to_all(content_derivative, 'head', split_axis=0, concat_axis=1, t...  14.3 us
    all_to_all x1, waiting for transfers between devices, local(): lax.all_to_all(key_heads, 'head', split_axis=1, concat_axis=0, tiled=True)  13.3 us
  transfers between devices with their start and end apart: 9, of which 8 were waited for; matrix products, arithmetic and copies ran while one was open for 37% of the time, Pallas kernels for 0%

commit v1 on v0

v1 whole, which is shorter than its diff:
```python
import functools
import math

import jax
import jax.numpy as jnp
from jax import lax
from jax.experimental import pallas as pl
from jax.experimental.pallas import tpu as pltpu
from jax.sharding import PartitionSpec as P

MESH = pl.DeviceIdType.MESH
F32 = jnp.float32
BF16 = jnp.bfloat16
NDOC = 16
HD = 128


def dot(a, b, ca, cb):
    return lax.dot_general(a, b, (((ca,), (cb,)), ((), ())), preferred_element_type=F32)


def kernel(
    dims, scaling,
    len_ref, q_ref, k_ref, v_ref, g_ref,
    oq_ref, ok_ref, ov_ref,
    toks, sums, arrived, totals, zgot, ready, entering, part, outs, mask_f, mask_b,
    ends, tab_p, tab_z,
    own_sem, xs_sem, xr_sem, is_sem, ir_sem, zs_sem, zr_sem, os_sem, or_sem, ys_sem, yr_sem, yl_sem,
):
    Z, Y, X, NH, TK = dims
    XY = X * Y
    CHUNKS = NH // XY
    CT = 2 * TK
    PT = XY * CT
    s = lax.axis_index("seq")
    hh = lax.axis_index("head")
    z, y = s // Y, s % Y
    x, c = hh // 2, hh % 2
    other = 1 - c
    me = y * X + x
    ins = (q_ref, k_ref, v_ref, g_ref)
    out_refs = (oq_ref, ok_ref, ov_ref)
    partner = (s, x * 2 + other)

    def at_plane(p):
        return (z * Y + p // X, (p % X) * 2 + c)

    def at_z(t):
        return (t * Y + y, hh)

    def ahead(i):
        return ((y + (i // X + i) % Y) % Y) * X + (x + i % X) % X

    def behind(i):
        return ((y - (i // X + i) % Y + Y) % Y) * X + (x - i % X + X) % X

    def z_step(n):
        return (z + ((n + 1) // 2) * (2 * (n % 2) - 1) + Z) % Z

    barrier = pltpu.get_barrier_semaphore()
    pl.semaphore_signal(barrier, inc=1, device_id=partner, device_id_type=MESH)

    def greet_plane(i, carry):
        pl.semaphore_signal(barrier, inc=1, device_id=at_plane(ahead(i)), device_id_type=MESH)
        return carry

    def greet_z(n, carry):
        pl.semaphore_signal(barrier, inc=1, device_id=at_z(z_step(n)), device_id_type=MESH)
        return carry

    lax.fori_loop(1, XY, greet_plane, 0)
    lax.fori_loop(1, Z, greet_z, 0)

    def own_copy(j, a):
        return pltpu.make_async_copy(
            ins[a].at[pl.ds(c * NH + j * XY, XY)],
            toks.at[a, pl.ds(j * XY, XY), c],
            own_sem.at[j, a],
        )

    def core_copy(j, a):
        return pltpu.make_async_remote_copy(
            src_ref=ins[a].at[pl.ds(other * NH + j * XY, XY)],
            dst_ref=toks.at[a, pl.ds(j * XY, XY), c],
            send_sem=xs_sem.at[j, a],
            recv_sem=xr_sem.at[j, a],
            device_id=partner,
            device_id_type=MESH,
        )

    def core_arrival(j, a):
        return pltpu.make_async_remote_copy(
            src_ref=ins[a].at[pl.ds(other * NH + j * XY, XY)],
            dst_ref=toks.at[a, pl.ds(j * XY, XY), other],
            send_sem=xs_sem.at[j, a],
            recv_sem=xr_sem.at[j, a],
            device_id=partner,
            device_id_type=MESH,
        )

    for j in range(CHUNKS):
        for a in range(4):
            own_copy(j, a).start()
    pl.semaphore_wait(barrier, XY + Z - 1)
    for j in range(CHUNKS):
        for a in range(4):
            core_copy(j, a).start()

    total_len = jnp.int32(0)
    for d in range(NDOC):
        total_len = total_len + len_ref[d]
        ends[d] = total_len

    def same(low, high):
        cut = jnp.int32(0)
        for d in range(NDOC):
            e = ends[d]
            cut = cut + jnp.where((low < e) & (e <= high), 1, 0)
        return jnp.where(cut == 0, 1.0, 0.0).astype(F32)

    def fill_plane(p, carry):
        first = z * PT + p * CT
        last = first + CT - 1
        tab_p[0, p] = same(first - 1, last)
        tab_p[1, p] = same(first - 1, first)
        tab_p[2, p] = same(first, last + 1)
        tab_p[3, p] = same(last, last + 1)
        return carry

    lax.fori_loop(0, XY, fill_plane, 0)

    def fill_z(t, carry):
        tab_z[0, t] = jnp.where(t < z, same((t + 1) * PT - 1, z * PT - 1), 0.0).astype(F32)
        tab_z[1, t] = jnp.where(t > z, same((z + 1) * PT, t * PT), 0.0).astype(F32)
        return carry

    lax.fori_loop(0, Z, fill_z, 0)

    base = (s * X + x) * CT
    rows = base + lax.broadcasted_iota(jnp.int32, (CT, CT), 0)
    cols = base + lax.broadcasted_iota(jnp.int32, (CT, CT), 1)
    row_doc = jnp.zeros((CT, CT), jnp.int32)
    col_doc = jnp.zeros((CT, CT), jnp.int32)
    first_doc = jnp.int32(0)
    last_doc = jnp.int32(0)
    for d in range(NDOC):
        e = ends[d]
        row_doc = row_doc + (e <= rows).astype(jnp.int32)
        col_doc = col_doc + (e <= cols).astype(jnp.int32)
        first_doc = first_doc + jnp.where(e <= base, 1, 0)
        last_doc = last_doc + jnp.where(e <= base + CT - 1, 1, 0)
    in_block = jnp.where((row_doc == col_doc) & (rows >= cols), scaling, 0.0).astype(F32)
    leading = jnp.where(row_doc == first_doc, 1.0, 0.0).astype(F32)
    trailing = jnp.where(row_doc == last_doc, 1.0, 0.0).astype(F32)
    mask_f[0] = in_block
    mask_f[1] = leading
    mask_f[2] = trailing
    mask_b[0] = leading.astype(BF16)
    mask_b[1] = trailing.astype(BF16)

    def tok(a, h):
        return toks[a, h].reshape(CT, HD)

    def send_sum(j, i):
        p = ahead(i)
        return pltpu.make_async_remote_copy(
            src_ref=sums.at[j * XY + p],
            dst_ref=arrived.at[j, me],
            send_sem=is_sem.at[j, i],
            recv_sem=ir_sem.at[j, me],
            device_id=at_plane(p),
            device_id_type=MESH,
        )

    def sum_arrival(j, i):
        p = behind(i)
        return pltpu.make_async_remote_copy(
            src_ref=sums.at[j * XY + p],
            dst_ref=arrived.at[j, p],
            send_sem=is_sem.at[j, i],
            recv_sem=ir_sem.at[j, p],
            device_id=at_plane(p),
            device_id_type=MESH,
        )

    def make_sums(j):
        def step(n, carry):
            i = n % XY
            h = j * XY + ahead(i)
            keys = tok(1, h) * mask_b[1]
            a_sum = (dot(tok(2, h), keys, 0, 0) * scaling).astype(BF16)
            queries = tok(0, h) * mask_b[0]
            b_sum = (dot(tok(3, h), queries, 0, 0) * scaling).astype(BF16)
            sums[h, 0] = a_sum
            sums[h, 1] = b_sum

            @pl.when(i == 0)
            def _():
                arrived[j, me, 0] = a_sum
                arrived[j, me, 1] = b_sum

            @pl.when(n >= 2)
            def _():
                send_sum(j, n - 1).start()

            return carry

        lax.fori_loop(1, XY + 1, step, 0)

    def local_work(j):
        def step(i, carry):
            h = j * XY + i
            q, k, v, g = (tok(a, h) for a in range(4))
            gs = (dot(g, v, 1, 1) * mask_f[0]).astype(BF16)
            sc = (dot(q, k, 1, 1) * mask_f[0]).astype(BF16)
            part[0, h] = dot(gs, k, 1, 0)
            part[1, h] = dot(gs, q, 0, 0)
            part[2, h] = dot(sc, g, 0, 0)
            return carry

        lax.fori_loop(0, XY, step, 0)

    def z_copy(j, n):
        t = z_step(n)
        return pltpu.make_async_remote_copy(
            src_ref=totals.at[j, jnp.where(t < z, 1, 0)],
            dst_ref=zgot.at[j, z],
            send_sem=zs_sem.at[j, n],
            recv_sem=zr_sem.at[j, z],
            device_id=at_z(t),
            device_id_type=MESH,
        )

    def z_arrival(j, t):
        return pltpu.make_async_remote_copy(
            src_ref=totals.at[j, 0],
            dst_ref=zgot.at[j, t],
            send_sem=zs_sem.at[j, 0],
            recv_sem=zr_sem.at[j, t],
            device_id=at_z(t),
            device_id_type=MESH,
        )

    def plane_totals(j):
        def wait_one(i, carry):
            sum_arrival(j, i).wait_recv()
            return carry

        lax.fori_loop(1, XY, wait_one, 0)

        def step(p, carry):
            a, b = carry
            r = XY - 1 - p
            a = tab_p[0, p] * a + arrived[j, p, 0].astype(F32)
            b = tab_p[2, r] * b + arrived[j, r, 1].astype(F32)
            return a, b

        zero = jnp.zeros((HD, HD), F32)
        a, b = lax.fori_loop(0, XY, step, (zero, zero))
        totals[j, 0] = a
        totals[j, 1] = b

    def send_totals(j):
        def step(n, carry):
            z_copy(j, n).start()
            return carry

        lax.fori_loop(1, Z, step, 0)

    def send_entering(j, i):
        p = ahead(i)
        return pltpu.make_async_remote_copy(
            src_ref=ready.at[j, p],
            dst_ref=entering.at[j * XY + me],
            send_sem=os_sem.at[j, i],
            recv_sem=or_sem.at[j, me],
            device_id=at_plane(p),
            device_id_type=MESH,
        )

    def entering_arrival(j, i):
        p = behind(i)
        return pltpu.make_async_remote_copy(
            src_ref=ready.at[j, p],
            dst_ref=entering.at[j * XY + p],
            send_sem=os_sem.at[j, i],
            recv_sem=or_sem.at[j, p],
            device_id=at_plane(p),
            device_id_type=MESH,
        )

    def make_entering(j):
        def add_plane(n, carry):
            a, b = carry
            t = z_step(n)
            z_arrival(j, t).wait_recv()
            got = zgot[j, t]
            return a + tab_z[0, t] * got, b + tab_z[1, t] * got

        zero = jnp.zeros((HD, HD), F32)
        start = lax.fori_loop(1, Z, add_plane, (zero, zero))

        def step(p, carry):
            a, b = carry
            r = XY - 1 - p
            ready[j, p, 0] = (tab_p[1, p] * a).astype(BF16)
            ready[j, r, 1] = (tab_p[3, r] * b).astype(BF16)
            a = tab_p[0, p] * a + arrived[j, p, 0].astype(F32)
            b = tab_p[2, r] * b + arrived[j, r, 1].astype(F32)
            return a, b

        lax.fori_loop(0, XY, step, start)
        entering[j * XY + me] = ready[j, me]

        def send(i, carry):
            send_entering(j, i).start()
            return carry

        lax.fori_loop(1, XY, send, 0)

    def finish(j):
        def step(i, carry):
            p = behind(i)
            h = j * XY + p

            @pl.when(i > 0)
            def _():
                entering_arrival(j, i).wait_recv()

            a = entering[h, 0]
            b = entering[h, 1]
            dq = part[0, h] + mask_f[1] * dot(tok(3, h), a, 1, 0)
            dk = part[1, h] + mask_f[2] * dot(tok(2, h), b, 1, 0)
            dv = part[2, h] + mask_f[2] * dot(tok(1, h), b, 1, 1)
            outs[0, h] = dq.astype(BF16).reshape(2, TK, HD)
            outs[1, h] = dk.astype(BF16).reshape(2, TK, HD)
            outs[2, h] = dv.astype(BF16).reshape(2, TK, HD)
            return carry

        lax.fori_loop(0, XY, step, 0)

    def out_own(j, a):
        return pltpu.make_async_copy(
            outs.at[a, pl.ds(j * XY, XY), c],
            out_refs[a].at[pl.ds(c * NH + j * XY, XY)],
            yl_sem.at[j, a],
        )

    def out_core(j, a):
        return pltpu.make_async_remote_copy(
            src_ref=outs.at[a, pl.ds(j * XY, XY), other],
            dst_ref=out_refs[a].at[pl.ds(c * NH + j * XY, XY)],
            send_sem=ys_sem.at[j, a],
            recv_sem=yr_sem.at[j, a],
            device_id=partner,
            device_id_type=MESH,
        )

    def out_arrival(j, a):
        return pltpu.make_async_remote_copy(
            src_ref=outs.at[a, pl.ds(j * XY, XY), other],
            dst_ref=out_refs[a].at[pl.ds(other * NH + j * XY, XY)],
            send_sem=ys_sem.at[j, a],
            recv_sem=yr_sem.at[j, a],
            device_id=partner,
            device_id_type=MESH,
        )

    for j in range(CHUNKS):
        for a in range(4):
            own_copy(j, a).wait()
            core_arrival(j, a).wait_recv()
        make_sums(j)
    local_work(0)
    for j in range(CHUNKS):
        plane_totals(j)
        if j + 1 < CHUNKS:
            send_totals(j)
            local_work(j + 1)
        else:
            send_totals(j)
    for j in range(CHUNKS):
        make_entering(j)
    for j in range(CHUNKS):
        finish(j)
        for a in range(3):
            out_own(j, a).start()
            out_core(j, a).start()

    for j in range(CHUNKS):
        for a in range(4):
            core_copy(j, a).wait_send()

        def drain(i, carry):
            send_sum(j, i).wait_send()
            send_entering(j, i).wait_send()
            return carry

        lax.fori_loop(1, XY, drain, 0)

        def drain_z(n, carry):
            z_copy(j, n).wait_send()
            return carry

        lax.fori_loop(1, Z, drain_z, 0)
        for a in range(3):
            out_own(j, a).wait()
            out_core(j, a).wait_send()
            out_arrival(j, a).wait_recv()


def exchange(dims, scaling, lengths, q, k, v, g):
    Z, Y, X, NH, TK = dims
    XY = X * Y
    CHUNKS = NH // XY
    CT = 2 * TK
    shape = jax.ShapeDtypeStruct((2 * NH, TK, HD), BF16)
    dma = pltpu.SemaphoreType.DMA
    return pl.pallas_call(
        functools.partial(kernel, dims, scaling),
        out_shape=(shape, shape, shape),
        in_specs=[pl.BlockSpec(memory_space=pltpu.SMEM)] + [pl.BlockSpec(memory_space=pl.ANY)] * 4,
        out_specs=(pl.BlockSpec(memory_space=pl.ANY),) * 3,
        scratch_shapes=[
            pltpu.VMEM((4, NH, 2, TK, HD), BF16),
            pltpu.VMEM((NH, 2, HD, HD), BF16),
            pltpu.VMEM((CHUNKS, XY, 2, HD, HD), BF16),
            pltpu.VMEM((CHUNKS, 2, HD, HD), F32),
            pltpu.VMEM((CHUNKS, Z, HD, HD), F32),
            pltpu.VMEM((CHUNKS, XY, 2, HD, HD), BF16),
            pltpu.VMEM((NH, 2, HD, HD), BF16),
            pltpu.VMEM((3, NH, CT, HD), F32),
            pltpu.VMEM((3, NH, 2, TK, HD), BF16),
            pltpu.VMEM((3, CT, HD), F32),
            pltpu.VMEM((2, CT, HD), BF16),
            pltpu.SMEM((NDOC,), jnp.int32),
            pltpu.SMEM((4, XY), F32),
            pltpu.SMEM((2, Z), F32),
            dma((CHUNKS, 4)),
            dma((CHUNKS, 4)),
            dma((CHUNKS, 4)),
            dma((CHUNKS, XY)),
            dma((CHUNKS, XY)),
            dma((CHUNKS, Z)),
            dma((CHUNKS, Z)),
            dma((CHUNKS, XY)),
            dma((CHUNKS, XY)),
            dma((CHUNKS, 3)),
            dma((CHUNKS, 3)),
            dma((CHUNKS, 3)),
        ],
        compiler_params=pltpu.CompilerParams(
            collective_id=0, has_side_effects=True, vmem_limit_bytes=56 << 20
        ),
    )(lengths, q, k, v, g)


def build(mesh, Z, Y, X):
    def local(queries, key_heads, value_heads, grad_output, doc_lengths):
        tokens, heads, width = queries.shape
        all_tokens = tokens * Z * Y * X * 2
        scaling = 1.0 / math.sqrt(width * (all_tokens // 2))
        dims = (Z, Y, X, heads // 2, tokens)
        by_head = [jnp.swapaxes(t, 0, 1) for t in (queries, key_heads, value_heads, grad_output)]
        results = exchange(dims, scaling, doc_lengths, *by_head)
        return tuple(jnp.swapaxes(t, 0, 1) for t in results)

    placed = P(("seq", "head"), None, None)
    return jax.shard_map(
        local,
        mesh=mesh,
        in_specs=(placed,) * 4 + (P(),),
        out_specs=(placed,) * 3,
        check_vma=False,
    )


def solution(mesh):
    return build(mesh, mesh.shape["seq"] // 4, 4, mesh.shape["head"] // 2)
```

time: 483 us -> 91.4 us (0.19)
  waiting for transfers between devices: 111 us -> 0 us
  other arithmetic: 99.8 us -> 0 us
  Pallas kernels: 0 us -> 77.2 us
  blocking collectives: 66.1 us -> 0 us
  local copies, waits for them, and re-layouts: 67.9 us -> 13.3 us
  starting transfers between devices: 44.6 us -> 0 us
  loops' own time: 41.8 us -> 0 us
  between operations: 27.1 us -> 0.67 us
  matrix products: 19.4 us -> 0 us
    select_n x64 -> x0, other arithmetic: 95.1 us -> none  [step(): return jax.tree.map(lambda a, b: jnp.where(reached, a, b), new, before)]
    pallas_call x0 -> x1, Pallas kernels: none -> 77.2 us  [exchange(): pl.pallas_call(functools.partial(kernel, dims, scaling), out_shape=(shape...]
    all_to_all x7 -> x0, waiting for transfers between devices: 71.3 us -> none  [the longest x1 13.3 us: local(): lax.all_to_all(key_heads, 'head', split_axis=1, concat_axis=0, tiled=True)]
    unnamed x1 -> x0, blocking collectives: 66.1 us -> none
    all_to_all x7 -> x0, starting transfers between devices: 44.6 us -> none  [the longest x1 14.3 us: local(): lax.all_to_all(content_derivative, 'head', split_axis=0, concat_axis=1, t...]
    another operation x2 -> x0, loops' own time: 41.8 us -> none  [entering(): return lax.fori_loop(0, count, step, start)]
    all_gather x2 -> x0, waiting for transfers between devices: 40.1 us -> none  [entering(): everything = jax.tree.map(lambda part: lax.all_gather(part, axis), value)]
    dynamic_slice x64 -> x0, local copies, waits for them, and re-layouts: 39.1 us -> none  [step(): new = combine(before, jax.tree.map(lambda part: part[at], everything))]
  transfers between devices with their start and end apart: 9 -> 0, of which waited for: 8 -> 0; matrix products, arithmetic and copies ran while one was open for 37% -> 0% of each run, Pallas kernels for 0% -> 0%
where the time goes in v1:
time: 91.4 us; the launch traced here: 91.2 us
  Pallas kernels  77.2 us (84%)
  local copies, waits for them, and re-layouts  13.3 us (15%)
    pallas_call x1, Pallas kernels, exchange(): pl.pallas_call(functools.partial(kernel, dims, scaling), out_shape=(shape...  77.2 us
    transpose x2, local copies, waits for them, and re-layouts, local(): jnp.swapaxes(t, 0, 1)  7.02 us
    unnamed x11, local copies, waits for them, and re-layouts  6.27 us

profile of v1, /device:TPU:1, one launch (start us, length us, event | category | flops | bytes accessed | tf_op | source)
XLA Modules:
  0.0 91.2 jit_solution(3708763274220617973)
XLA Ops:
  0.6 0.0 copy-start.2
  0.6 0.0 copy-start.3
  0.7 4.4 %copy_bitcast_fusion.2 = (bf16[64,64,128]{2,1,0:T(8,128)(2,1)}, bf16[64,64,128]{2,1,0:T(8,128)(2,1)}) fusion(bf16[64,64,128]{2,1,0:T(8,128)(2,1)} %param.6, bf16[64,64,128]{2,1,0:T(8,128)(2,1)} %param.5), kind=kLoop, calls=%fused_computation.2 | loop fusion | bytes 4194304 | tf_op jit(solution)/shard_map/transpose | solution.py:464
  5.0 0.0 copy-done.2
  5.0 0.0 copy-done.3
  5.0 2.7 %copy_bitcast_fusion = (bf16[64,64,128]{2,1,0:T(8,128)(2,1)}, bf16[64,64,128]{2,1,0:T(8,128)(2,1)}) fusion(bf16[64,64,128]{2,1,0:T(8,128)(2,1)S(1)} %copy-done.2, bf16[64,64,128]{2,1,0:T(8,128)(2,1)S(1)} %copy-done.3), kind=kLoop, calls=%fused_computation | loop fusion | bytes 4194304 | tf_op jit(solution)/shard_map/transpose | solution.py:464
  7.7 77.2 %shard_map.76 = (bf16[64,64,128]{2,1,0:T(8,128)(2,1)}, bf16[64,64,128]{2,1,0:T(8,128)(2,1)}, bf16[64,64,128]{2,1,0:T(8,128)(2,1)}) custom-call(s32[16]{0:T(128)} %len_ref.1, bf16[64,64,128]{2,1,0:T(8,128)(2,1)} %get-tuple-element.15.q_ref, bf16[64,64,128]{2,1,0:T(8,128)(2,1)} %get-tuple-element.14.k_ref, bf16[64,64,128]{2,1,0:T(8,128)(2,1)} %get-tuple-element.13.v_ref, ...), custom_call_target="tpu_custom_call" | custom-call | tf_op jit(solution)/shard_map/pallas_call | solution.py:419
  84.9 0.0 copy-start.1
  84.9 3.0 %copy.12 = bf16[64,64,128]{2,1,0:T(8,128)(2,1)} copy(bf16[64,64,128]{2,0,1:T(8,128)(2,1)} %bitcast.13) | data formatting | bytes 2097152
  87.9 0.0 copy-done.1
  87.9 0.0 copy-start
  87.9 1.6 %copy.13 = bf16[64,64,128]{2,1,0:T(8,128)(2,1)} copy(bf16[64,64,128]{2,0,1:T(8,128)(2,1)S(1)} %bitcast.12) | data formatting | bytes 2097152
  89.5 0.0 copy-done
  89.5 1.6 %copy.14 = bf16[64,64,128]{2,1,0:T(8,128)(2,1)} copy(bf16[64,64,128]{2,0,1:T(8,128)(2,1)S(1)} %bitcast.11) | data formatting | bytes 2097152
Async XLA Ops:
  0.6 4.4 %copy-start.2 = (bf16[64,64,128]{2,1,0:T(8,128)(2,1)S(1)}, bf16[64,64,128]{2,1,0:T(8,128)(2,1)}, u32[]{:S(2)}) copy-start(bf16[64,64,128]{2,1,0:T(8,128)(2,1)} %param.8) | copy-start | bytes 3145732
  0.6 4.4 %copy-start.3 = (bf16[64,64,128]{2,1,0:T(8,128)(2,1)S(1)}, bf16[64,64,128]{2,1,0:T(8,128)(2,1)}, u32[]{:S(2)}) copy-start(bf16[64,64,128]{2,1,0:T(8,128)(2,1)} %param.7) | copy-start | bytes 3145732
  84.9 3.0 %copy-start.1 = (bf16[64,64,128]{2,1,0:T(8,128)(2,1)S(1)}, bf16[64,64,128]{2,1,0:T(8,128)(2,1)}, u32[]{:S(2)}) copy-start(bf16[64,64,128]{2,1,0:T(8,128)(2,1)} %get-tuple-element.7) | copy-start | bytes 3145732
  87.9 1.7 %copy-start = (bf16[64,64,128]{2,1,0:T(8,128)(2,1)S(1)}, bf16[64,64,128]{2,1,0:T(8,128)(2,1)}, u32[]{:S(2)}) copy-start(bf16[64,64,128]{2,1,0:T(8,128)(2,1)} %get-tuple-element.8) | copy-start | bytes 3145732

commit v2 on v1

--- a/solution.py
+++ b/solution.py
@@ -23,13 +23,15 @@
     dims, scaling,
     len_ref, q_ref, k_ref, v_ref, g_ref,
     oq_ref, ok_ref, ov_ref,
-    toks, sums, arrived, totals, zgot, ready, entering, part, outs, mask_f, mask_b,
+    raw, toks, sums, arrived, totals, zgot, ready, entering, part, outs, swapped, mask_f, mask_b,
     ends, tab_p, tab_z,
     own_sem, xs_sem, xr_sem, is_sem, ir_sem, zs_sem, zr_sem, os_sem, or_sem, ys_sem, yr_sem, yl_sem,
 ):
     Z, Y, X, NH, TK = dims
     XY = X * Y
     CHUNKS = NH // XY
+    PARTS = 2 * CHUNKS
+    HALF = HD // 2
     CT = 2 * TK
     PT = XY * CT
     s = lax.axis_index("seq")
@@ -73,15 +75,15 @@
 
     def own_copy(j, a):
         return pltpu.make_async_copy(
-            ins[a].at[pl.ds(c * NH + j * XY, XY)],
-            toks.at[a, pl.ds(j * XY, XY), c],
+            ins[a].at[:, pl.ds(pl.multiple_of(c * NH + j * XY, 8), XY)],
+            raw.at[a, j, c],
             own_sem.at[j, a],
         )
 
     def core_copy(j, a):
         return pltpu.make_async_remote_copy(
-            src_ref=ins[a].at[pl.ds(other * NH + j * XY, XY)],
-            dst_ref=toks.at[a, pl.ds(j * XY, XY), c],
+            src_ref=ins[a].at[:, pl.ds(pl.multiple_of(other * NH + j * XY, 8), XY)],
+            dst_ref=raw.at[a, j, c],
             send_sem=xs_sem.at[j, a],
             recv_sem=xr_sem.at[j, a],
             device_id=partner,
@@ -90,8 +92,8 @@
 
     def core_arrival(j, a):
         return pltpu.make_async_remote_copy(
-            src_ref=ins[a].at[pl.ds(other * NH + j * XY, XY)],
-            dst_ref=toks.at[a, pl.ds(j * XY, XY), other],
+            src_ref=ins[a].at[:, pl.ds(pl.multiple_of(other * NH + j * XY, 8), XY)],
+            dst_ref=raw.at[a, j, other],
             send_sem=xs_sem.at[j, a],
             recv_sem=xr_sem.at[j, a],
             device_id=partner,
@@ -127,14 +129,10 @@
         tab_p[3, p] = same(last, last + 1)
         return carry
 
-    lax.fori_loop(0, XY, fill_plane, 0)
-
     def fill_z(t, carry):
         tab_z[0, t] = jnp.where(t < z, same((t + 1) * PT - 1, z * PT - 1), 0.0).astype(F32)
         tab_z[1, t] = jnp.where(t > z, same((z + 1) * PT, t * PT), 0.0).astype(F32)
         return carry
-
-    lax.fori_loop(0, Z, fill_z, 0)
 
     base = (s * X + x) * CT
     rows = base + lax.broadcasted_iota(jnp.int32, (CT, CT), 0)
@@ -161,24 +159,28 @@
     def tok(a, h):
         return toks[a, h].reshape(CT, HD)
 
-    def send_sum(j, i):
+    def swap_in(j, core):
+        for a in range(4):
+            toks[a, pl.ds(j * XY, XY), core] = jnp.swapaxes(raw[a, j, core], 0, 1)
+
+    def send_sum(u, i):
         p = ahead(i)
         return pltpu.make_async_remote_copy(
-            src_ref=sums.at[j * XY + p],
-            dst_ref=arrived.at[j, me],
-            send_sem=is_sem.at[j, i],
-            recv_sem=ir_sem.at[j, me],
+            src_ref=sums.at[(u // 2) * XY + p, u % 2],
+            dst_ref=arrived.at[u, me],
+            send_sem=is_sem.at[u, i],
+            recv_sem=ir_sem.at[u, me],
             device_id=at_plane(p),
             device_id_type=MESH,
         )
 
-    def sum_arrival(j, i):
+    def sum_arrival(u, i):
         p = behind(i)
         return pltpu.make_async_remote_copy(
-            src_ref=sums.at[j * XY + p],
-            dst_ref=arrived.at[j, p],
-            send_sem=is_sem.at[j, i],
-            recv_sem=ir_sem.at[j, p],
+            src_ref=sums.at[(u // 2) * XY + p, u % 2],
+            dst_ref=arrived.at[u, p],
+            send_sem=is_sem.at[u, i],
+            recv_sem=ir_sem.at[u, p],
             device_id=at_plane(p),
             device_id_type=MESH,
         )
@@ -188,28 +190,35 @@
             i = n % XY
             h = j * XY + ahead(i)
             keys = tok(1, h) * mask_b[1]
-            a_sum = (dot(tok(2, h), keys, 0, 0) * scaling).astype(BF16)
+            a_sum = (dot(tok(2, h), keys, 0, 0) * scaling).astype(BF16).reshape(2, HALF, HD)
             queries = tok(0, h) * mask_b[0]
-            b_sum = (dot(tok(3, h), queries, 0, 0) * scaling).astype(BF16)
-            sums[h, 0] = a_sum
-            sums[h, 1] = b_sum
+            b_sum = (dot(tok(3, h), queries, 0, 0) * scaling).astype(BF16).reshape(2, HALF, HD)
+            for r in range(2):
+                sums[h, r, 0] = a_sum[r]
+                sums[h, r, 1] = b_sum[r]
 
             @pl.when(i == 0)
             def _():
-                arrived[j, me, 0] = a_sum
-                arrived[j, me, 1] = b_sum
+                for r in range(2):
+                    arrived[2 * j + r, me, 0] = a_sum[r]
+                    arrived[2 * j + r, me, 1] = b_sum[r]
 
             @pl.when(n >= 2)
             def _():
-                send_sum(j, n - 1).start()
+                send_sum(2 * j, n - 1).start()
 
             return carry
 
         lax.fori_loop(1, XY + 1, step, 0)
 
-    def local_work(j):
-        def step(i, carry):
-            h = j * XY + i
+        def send_rest(i, carry):
+            send_sum(2 * j + 1, i).start()
+            return carry
+
+        lax.fori_loop(1, XY, send_rest, 0)
+
+    def local_work(low, high):
+        def step(h, carry):
             q, k, v, g = (tok(a, h) for a in range(4))
             gs = (dot(g, v, 1, 1) * mask_f[0]).astype(BF16)
             sc = (dot(q, k, 1, 1) * mask_f[0]).astype(BF16)
@@ -218,7 +227,7 @@
             part[2, h] = dot(sc, g, 0, 0)
             return carry
 
-        lax.fori_loop(0, XY, step, 0)
+        lax.fori_loop(low, high, step, 0)
 
     def z_copy(j, n):
         t = z_step(n)
@@ -255,7 +264,7 @@
             b = tab_p[2, r] * b + arrived[j, r, 1].astype(F32)
             return a, b
 
-        zero = jnp.zeros((HD, HD), F32)
+        zero = jnp.zeros((HALF, HD), F32)
         a, b = lax.fori_loop(0, XY, step, (zero, zero))
         totals[j, 0] = a
         totals[j, 1] = b
@@ -271,7 +280,7 @@
         p = ahead(i)
         return pltpu.make_async_remote_copy(
             src_ref=ready.at[j, p],
-            dst_ref=entering.at[j * XY + me],
+            dst_ref=entering.at[(j // 2) * XY + me, j % 2],
             send_sem=os_sem.at[j, i],
             recv_sem=or_sem.at[j, me],
             device_id=at_plane(p),
@@ -282,7 +291,7 @@
         p = behind(i)
         return pltpu.make_async_remote_copy(
             src_ref=ready.at[j, p],
-            dst_ref=entering.at[j * XY + p],
+            dst_ref=entering.at[(j // 2) * XY + p, j % 2],
             send_sem=os_sem.at[j, i],
             recv_sem=or_sem.at[j, p],
             device_id=at_plane(p),
@@ -297,7 +306,7 @@
             got = zgot[j, t]
             return a + tab_z[0, t] * got, b + tab_z[1, t] * got
 
-        zero = jnp.zeros((HD, HD), F32)
+        zero = jnp.zeros((HALF, HD), F32)
         start = lax.fori_loop(1, Z, add_plane, (zero, zero))
 
         def step(p, carry):
@@ -310,7 +319,7 @@
             return a, b
 
         lax.fori_loop(0, XY, step, start)
-        entering[j * XY + me] = ready[j, me]
+        entering[(j // 2) * XY + me, j % 2] = ready[j, me]
 
         def send(i, carry):
             send_entering(j, i).start()
@@ -325,10 +334,11 @@
 
             @pl.when(i > 0)
             def _():
-                entering_arrival(j, i).wait_recv()
-
-            a = entering[h, 0]
-            b = entering[h, 1]
+                entering_arrival(2 * j, i).wait_recv()
+                entering_arrival(2 * j + 1, i).wait_recv()
+
+            a = entering[h, :, 0].reshape(HD, HD)
+            b = entering[h, :, 1].reshape(HD, HD)
             dq = part[0, h] + mask_f[1] * dot(tok(3, h), a, 1, 0)
             dk = part[1, h] + mask_f[2] * dot(tok(2, h), b, 1, 0)
             dv = part[2, h] + mask_f[2] * dot(tok(1, h), b, 1, 1)
@@ -338,18 +348,21 @@
             return carry
 
         lax.fori_loop(0, XY, step, 0)
+        for a in range(3):
+            for core in range(2):
+                swapped[a, j, core] = jnp.swapaxes(outs[a, pl.ds(j * XY, XY), core], 0, 1)
 
     def out_own(j, a):
         return pltpu.make_async_copy(
-            outs.at[a, pl.ds(j * XY, XY), c],
-            out_refs[a].at[pl.ds(c * NH + j * XY, XY)],
+            swapped.at[a, j, c],
+            out_refs[a].at[:, pl.ds(pl.multiple_of(c * NH + j * XY, 8), XY)],
             yl_sem.at[j, a],
         )
 
     def out_core(j, a):
         return pltpu.make_async_remote_copy(
-            src_ref=outs.at[a, pl.ds(j * XY, XY), other],
-            dst_ref=out_refs[a].at[pl.ds(c * NH + j * XY, XY)],
+            src_ref=swapped.at[a, j, other],
+            dst_ref=out_refs[a].at[:, pl.ds(pl.multiple_of(c * NH + j * XY, 8), XY)],
             send_sem=ys_sem.at[j, a],
             recv_sem=yr_sem.at[j, a],
             device_id=partner,
@@ -358,8 +371,8 @@
 
     def out_arrival(j, a):
         return pltpu.make_async_remote_copy(
-            src_ref=outs.at[a, pl.ds(j * XY, XY), other],
-            dst_ref=out_refs[a].at[pl.ds(other * NH + j * XY, XY)],
+            src_ref=swapped.at[a, j, other],
+            dst_ref=out_refs[a].at[:, pl.ds(pl.multiple_of(other * NH + j * XY, 8), XY)],
             send_sem=ys_sem.at[j, a],
             recv_sem=yr_sem.at[j, a],
             device_id=partner,
@@ -369,40 +382,50 @@
     for j in range(CHUNKS):
         for a in range(4):
             own_copy(j, a).wait()
+        swap_in(j, c)
+    for j in range(CHUNKS):
+        for a in range(4):
             core_arrival(j, a).wait_recv()
+        swap_in(j, other)
         make_sums(j)
-    local_work(0)
-    for j in range(CHUNKS):
-        plane_totals(j)
-        if j + 1 < CHUNKS:
-            send_totals(j)
-            local_work(j + 1)
-        else:
-            send_totals(j)
-    for j in range(CHUNKS):
-        make_entering(j)
+    lax.fori_loop(0, XY, fill_plane, 0)
+    lax.fori_loop(0, Z, fill_z, 0)
+
+    def gather(u):
+        plane_totals(u)
+        send_totals(u)
+
+    piece = NH // PARTS
+    for u in range(PARTS):
+        local_work(u * piece, (u + 1) * piece)
+        gather(u)
+        if u >= 2:
+            make_entering(u - 2)
+    make_entering(PARTS - 2)
+    make_entering(PARTS - 1)
     for j in range(CHUNKS):
         finish(j)
         for a in range(3):
             out_own(j, a).start()
             out_core(j, a).start()
 
+    for u in range(PARTS):
+
+        def drain(i, carry):
+            send_sum(u, i).wait_send()
+            send_entering(u, i).wait_send()
+            return carry
+
+        lax.fori_loop(1, XY, drain, 0)
+
+        def drain_z(n, carry):
+            z_copy(u, n).wait_send()
+            return carry
+
+        lax.fori_loop(1, Z, drain_z, 0)
     for j in range(CHUNKS):
         for a in range(4):
             core_copy(j, a).wait_send()
-
-        def drain(i, carry):
-            send_sum(j, i).wait_send()
-            send_entering(j, i).wait_send()
-            return carry
-
-        lax.fori_loop(1, XY, drain, 0)
-
-        def drain_z(n, carry):
-            z_copy(j, n).wait_send()
-            return carry
-
-        lax.fori_loop(1, Z, drain_z, 0)
         for a in range(3):
             out_own(j, a).wait()
             out_core(j, a).wait_send()
@@ -414,7 +437,9 @@
     XY = X * Y
     CHUNKS = NH // XY
     CT = 2 * TK
-    shape = jax.ShapeDtypeStruct((2 * NH, TK, HD), BF16)
+    PARTS = 2 * CHUNKS
+    HALF = HD // 2
+    shape = jax.ShapeDtypeStruct((TK, 2 * NH, HD), BF16)
     dma = pltpu.SemaphoreType.DMA
     return pl.pallas_call(
         functools.partial(kernel, dims, scaling),
@@ -422,15 +447,17 @@
         in_specs=[pl.BlockSpec(memory_space=pltpu.SMEM)] + [pl.BlockSpec(memory_space=pl.ANY)] * 4,
         out_specs=(pl.BlockSpec(memory_space=pl.ANY),) * 3,
         scratch_shapes=[
+            pltpu.VMEM((4, CHUNKS, 2, TK, XY, HD), BF16),
             pltpu.VMEM((4, NH, 2, TK, HD), BF16),
-            pltpu.VMEM((NH, 2, HD, HD), BF16),
-            pltpu.VMEM((CHUNKS, XY, 2, HD, HD), BF16),
-            pltpu.VMEM((CHUNKS, 2, HD, HD), F32),
-            pltpu.VMEM((CHUNKS, Z, HD, HD), F32),
-            pltpu.VMEM((CHUNKS, XY, 2, HD, HD), BF16),
-            pltpu.VMEM((NH, 2, HD, HD), BF16),
+            pltpu.VMEM((NH, 2, 2, HALF, HD), BF16),
+            pltpu.VMEM((PARTS, XY, 2, HALF, HD), BF16),
+            pltpu.VMEM((PARTS, 2, HALF, HD), F32),
+            pltpu.VMEM((PARTS, Z, HALF, HD), F32),
+            pltpu.VMEM((PARTS, XY, 2, HALF, HD), BF16),
+            pltpu.VMEM((NH, 2, 2, HALF, HD), BF16),
             pltpu.VMEM((3, NH, CT, HD), F32),
             pltpu.VMEM((3, NH, 2, TK, HD), BF16),
+            pltpu.VMEM((3, CHUNKS, 2, TK, XY, HD), BF16),
             pltpu.VMEM((3, CT, HD), F32),
             pltpu.VMEM((2, CT, HD), BF16),
             pltpu.SMEM((NDOC,), jnp.int32),
@@ -439,12 +466,12 @@
             dma((CHUNKS, 4)),
             dma((CHUNKS, 4)),
             dma((CHUNKS, 4)),
-            dma((CHUNKS, XY)),
-            dma((CHUNKS, XY)),
-            dma((CHUNKS, Z)),
-            dma((CHUNKS, Z)),
-            dma((CHUNKS, XY)),
-            dma((CHUNKS, XY)),
+            dma((PARTS, XY)),
+            dma((PARTS, XY)),
+            dma((PARTS, Z)),
+            dma((PARTS, Z)),
+            dma((PARTS, XY)),
+            dma((PARTS, XY)),
             dma((CHUNKS, 3)),
             dma((CHUNKS, 3)),
             dma((CHUNKS, 3)),
@@ -461,9 +488,7 @@
         all_tokens = tokens * Z * Y * X * 2
         scaling = 1.0 / math.sqrt(width * (all_tokens // 2))
         dims = (Z, Y, X, heads // 2, tokens)
-        by_head = [jnp.swapaxes(t, 0, 1) for t in (queries, key_heads, value_heads, grad_output)]
-        results = exchange(dims, scaling, doc_lengths, *by_head)
-        return tuple(jnp.swapaxes(t, 0, 1) for t in results)
+        return exchange(dims, scaling, doc_lengths, queries, key_heads, value_heads, grad_output)
 
     placed = P(("seq", "head"), None, None)
     return jax.shard_map(

time: 91.4 us -> 77.4 us (0.85)
  local copies, waits for them, and re-layouts: 13.3 us -> 4.93 us
  Pallas kernels: 77.2 us -> 71.6 us
    transpose x2 -> x0, local copies, waits for them, and re-layouts: 7.02 us -> none  [local(): jnp.swapaxes(t, 0, 1)]
    pallas_call x1, Pallas kernels: 77.2 us -> 71.6 us  [exchange(): pl.pallas_call(functools.partial(kernel, dims, scaling), out_shape=(shape...]
    unnamed x11 -> x7, local copies, waits for them, and re-layouts: 6.27 us -> 4.93 us
where the time goes in v2:
time: 77.4 us; the launch traced here: 77.2 us
  Pallas kernels  71.6 us (93%)
  local copies, waits for them, and re-layouts  4.93 us (6%)
    pallas_call x1, Pallas kernels, exchange(): pl.pallas_call(functools.partial(kernel, dims, scaling), out_shape=(shape...  71.6 us
    unnamed x7, local copies, waits for them, and re-layouts  4.93 us

profile of v2, /device:TPU:1, one launch (start us, length us, event | category | flops | bytes accessed | tf_op | source)
XLA Modules:
  0.0 77.2 jit_solution(16650324671038413844)
XLA Ops:
  0.6 71.6 %shard_map.76 = (bf16[64,64,128]{2,1,0:T(8,128)(2,1)}, bf16[64,64,128]{2,1,0:T(8,128)(2,1)}, bf16[64,64,128]{2,1,0:T(8,128)(2,1)}) custom-call(s32[16]{0:T(128)} %len_ref.1, bf16[64,64,128]{2,1,0:T(8,128)(2,1)} %q_ref.1, bf16[64,64,128]{2,1,0:T(8,128)(2,1)} %k_ref.1, bf16[64,64,128]{2,1,0:T(8,128)(2,1)} %v_ref.1, bf16[64,64,128]{2,1,0:T(8,128)(2,1)} %g_ref.1), custom_call_target="tpu_custom_call" | custom-call | tf_op jit(solution)/shard_map/pallas_call | solution.py:444
  72.3 0.0 copy-start.1
  72.3 2.4 %copy.11 = bf16[64,64,128]{2,1,0:T(8,128)(2,1)} copy(bf16[64,64,128]{2,1,0:T(8,128)(2,1)} %get-tuple-element.6) | data formatting | bytes 2097152
  74.6 0.0 copy-done.1
  74.6 0.0 copy-start
  74.6 1.0 %copy.12 = bf16[64,64,128]{2,1,0:T(8,128)(2,1)} copy(bf16[64,64,128]{2,1,0:T(8,128)(2,1)S(1)} %copy-done.1) | data formatting | bytes 2097152
  75.6 0.6 copy-done
  76.2 1.0 %copy.13 = bf16[64,64,128]{2,1,0:T(8,128)(2,1)} copy(bf16[64,64,128]{2,1,0:T(8,128)(2,1)S(1)} %copy-done) | data formatting | bytes 2097152
Async XLA Ops:
  72.3 2.4 %copy-start.1 = (bf16[64,64,128]{2,1,0:T(8,128)(2,1)S(1)}, bf16[64,64,128]{2,1,0:T(8,128)(2,1)}, u32[]{:S(2)}) copy-start(bf16[64,64,128]{2,1,0:T(8,128)(2,1)} %get-tuple-element.7) | copy-start | bytes 3145732
  74.6 1.6 %copy-start = (bf16[64,64,128]{2,1,0:T(8,128)(2,1)S(1)}, bf16[64,64,128]{2,1,0:T(8,128)(2,1)}, u32[]{:S(2)}) copy-start(bf16[64,64,128]{2,1,0:T(8,128)(2,1)} %get-tuple-element.8) | copy-start | bytes 3145732

commit v3 on v2

--- a/solution.py
+++ b/solution.py
@@ -15,6 +15,14 @@
 HD = 128
 
 
+STEPS = (
+    (0, 0), (2, 2), (3, 2), (2, 3), (1, 2), (2, 1), (0, 2), (2, 0),
+    (3, 1), (1, 3), (3, 3), (1, 1), (0, 3), (3, 0), (0, 1), (1, 0),
+)
+STEPS_X = sum(dx << (2 * i) for i, (dx, dy) in enumerate(STEPS))
+STEPS_Y = sum(dy << (2 * i) for i, (dx, dy) in enumerate(STEPS))
+
+
 def dot(a, b, ca, cb):
     return lax.dot_general(a, b, (((ca,), (cb,)), ((), ())), preferred_element_type=F32)
 
@@ -25,7 +33,7 @@
     oq_ref, ok_ref, ov_ref,
     raw, toks, sums, arrived, totals, zgot, ready, entering, part, outs, swapped, mask_f, mask_b,
     ends, tab_p, tab_z,
-    own_sem, xs_sem, xr_sem, is_sem, ir_sem, zs_sem, zr_sem, os_sem, or_sem, ys_sem, yr_sem, yl_sem,
+    own_sem, xs_sem, xr_sem, is_sem, ir_sem, zs_sem, zr_sem, os_sem, or_sem, last_sem, ys_sem, yr_sem, yl_sem,
 ):
     Z, Y, X, NH, TK = dims
     XY = X * Y
@@ -50,28 +58,35 @@
     def at_z(t):
         return (t * Y + y, hh)
 
+    def plane_step(dx, dy):
+        return (z * Y + (y + dy) % Y, ((x + dx) % X) * 2 + c)
+
+    def offset(i):
+        return (STEPS_X >> (2 * i)) & 3, (STEPS_Y >> (2 * i)) & 3
+
     def ahead(i):
-        return ((y + (i // X + i) % Y) % Y) * X + (x + i % X) % X
+        dx, dy = offset(i)
+        return ((y + dy) % Y) * X + (x + dx) % X
 
     def behind(i):
-        return ((y - (i // X + i) % Y + Y) % Y) * X + (x - i % X + X) % X
+        dx, dy = offset(i)
+        return ((y - dy + Y) % Y) * X + (x - dx + X) % X
 
     def z_step(n):
-        return (z + ((n + 1) // 2) * (2 * (n % 2) - 1) + Z) % Z
+        return (z + (((n + 1) // 2) if n % 2 else Z - n // 2)) % Z
 
     barrier = pltpu.get_barrier_semaphore()
-    pl.semaphore_signal(barrier, inc=1, device_id=partner, device_id_type=MESH)
-
-    def greet_plane(i, carry):
-        pl.semaphore_signal(barrier, inc=1, device_id=at_plane(ahead(i)), device_id_type=MESH)
-        return carry
-
-    def greet_z(n, carry):
-        pl.semaphore_signal(barrier, inc=1, device_id=at_z(z_step(n)), device_id_type=MESH)
-        return carry
-
-    lax.fori_loop(1, XY, greet_plane, 0)
-    lax.fori_loop(1, Z, greet_z, 0)
+
+    def greet(device):
+        pl.semaphore_signal(barrier, inc=1, device_id=device, device_id_type=MESH)
+
+    for n in range(Z - 1, 3, -1):
+        greet(at_z(z_step(n)))
+    for dx, dy in STEPS[1:]:
+        greet(plane_step(dx, dy))
+    for n in range(3, 0, -1):
+        greet(at_z(z_step(n)))
+    greet(partner)
 
     def own_copy(j, a):
         return pltpu.make_async_copy(
@@ -103,10 +118,6 @@
     for j in range(CHUNKS):
         for a in range(4):
             own_copy(j, a).start()
-    pl.semaphore_wait(barrier, XY + Z - 1)
-    for j in range(CHUNKS):
-        for a in range(4):
-            core_copy(j, a).start()
 
     total_len = jnp.int32(0)
     for d in range(NDOC):
@@ -168,20 +179,20 @@
         return pltpu.make_async_remote_copy(
             src_ref=sums.at[(u // 2) * XY + p, u % 2],
             dst_ref=arrived.at[u, me],
-            send_sem=is_sem.at[u, i],
-            recv_sem=ir_sem.at[u, me],
+            send_sem=is_sem.at[u],
+            recv_sem=ir_sem.at[u],
             device_id=at_plane(p),
             device_id_type=MESH,
         )
 
-    def sum_arrival(u, i):
-        p = behind(i)
-        return pltpu.make_async_remote_copy(
-            src_ref=sums.at[(u // 2) * XY + p, u % 2],
-            dst_ref=arrived.at[u, p],
-            send_sem=is_sem.at[u, i],
-            recv_sem=ir_sem.at[u, p],
-            device_id=at_plane(p),
+    def all_sums(u):
+        block = arrived.at[u, pl.ds(0, XY - 1)]
+        return pltpu.make_async_remote_copy(
+            src_ref=block,
+            dst_ref=block,
+            send_sem=is_sem.at[u],
+            recv_sem=ir_sem.at[u],
+            device_id=partner,
             device_id_type=MESH,
         )
 
@@ -211,11 +222,8 @@
 
         lax.fori_loop(1, XY + 1, step, 0)
 
-        def send_rest(i, carry):
+        for i in range(1, XY):
             send_sum(2 * j + 1, i).start()
-            return carry
-
-        lax.fori_loop(1, XY, send_rest, 0)
 
     def local_work(low, high):
         def step(h, carry):
@@ -229,33 +237,30 @@
 
         lax.fori_loop(low, high, step, 0)
 
-    def z_copy(j, n):
+    def z_copy(u, n):
         t = z_step(n)
         return pltpu.make_async_remote_copy(
-            src_ref=totals.at[j, jnp.where(t < z, 1, 0)],
-            dst_ref=zgot.at[j, z],
-            send_sem=zs_sem.at[j, n],
-            recv_sem=zr_sem.at[j, z],
+            src_ref=totals.at[u, jnp.where(t < z, 1, 0)],
+            dst_ref=zgot.at[u, z],
+            send_sem=zs_sem.at[u],
+            recv_sem=zr_sem.at[u],
             device_id=at_z(t),
             device_id_type=MESH,
         )
 
-    def z_arrival(j, t):
-        return pltpu.make_async_remote_copy(
-            src_ref=totals.at[j, 0],
-            dst_ref=zgot.at[j, t],
-            send_sem=zs_sem.at[j, 0],
-            recv_sem=zr_sem.at[j, t],
-            device_id=at_z(t),
+    def all_z(u):
+        block = zgot.at[u, pl.ds(0, Z - 1)]
+        return pltpu.make_async_remote_copy(
+            src_ref=block,
+            dst_ref=block,
+            send_sem=zs_sem.at[u],
+            recv_sem=zr_sem.at[u],
+            device_id=partner,
             device_id_type=MESH,
         )
 
     def plane_totals(j):
-        def wait_one(i, carry):
-            sum_arrival(j, i).wait_recv()
-            return carry
-
-        lax.fori_loop(1, XY, wait_one, 0)
+        all_sums(j).wait_recv()
 
         def step(p, carry):
             a, b = carry
@@ -270,44 +275,52 @@
         totals[j, 1] = b
 
     def send_totals(j):
-        def step(n, carry):
+        for n in range(1, Z):
             z_copy(j, n).start()
-            return carry
-
-        lax.fori_loop(1, Z, step, 0)
-
-    def send_entering(j, i):
+
+    def entering_sem(u, p):
+        return last_sem.at[p] if u == PARTS - 1 else or_sem.at[u]
+
+    def send_entering(u, i):
         p = ahead(i)
         return pltpu.make_async_remote_copy(
-            src_ref=ready.at[j, p],
-            dst_ref=entering.at[(j // 2) * XY + me, j % 2],
-            send_sem=os_sem.at[j, i],
-            recv_sem=or_sem.at[j, me],
+            src_ref=ready.at[u, p],
+            dst_ref=entering.at[(u // 2) * XY + me, u % 2],
+            send_sem=os_sem.at[u],
+            recv_sem=entering_sem(u, me),
             device_id=at_plane(p),
             device_id_type=MESH,
         )
 
-    def entering_arrival(j, i):
-        p = behind(i)
-        return pltpu.make_async_remote_copy(
-            src_ref=ready.at[j, p],
-            dst_ref=entering.at[(j // 2) * XY + p, j % 2],
-            send_sem=os_sem.at[j, i],
-            recv_sem=or_sem.at[j, p],
+    def last_entering(p):
+        u = PARTS - 1
+        return pltpu.make_async_remote_copy(
+            src_ref=ready.at[u, p],
+            dst_ref=entering.at[(u // 2) * XY + p, u % 2],
+            send_sem=os_sem.at[u],
+            recv_sem=entering_sem(u, p),
             device_id=at_plane(p),
             device_id_type=MESH,
         )
 
+    def all_entering(u):
+        block = ready.at[u, pl.ds(0, XY - 1)]
+        return pltpu.make_async_remote_copy(
+            src_ref=block,
+            dst_ref=block,
+            send_sem=os_sem.at[u],
+            recv_sem=or_sem.at[min(u, PARTS - 2)],
+            device_id=partner,
+            device_id_type=MESH,
+        )
+
     def make_entering(j):
-        def add_plane(n, carry):
-            a, b = carry
+        all_z(j).wait_recv()
+        start = (jnp.zeros((HALF, HD), F32), jnp.zeros((HALF, HD), F32))
+        for n in range(1, Z):
             t = z_step(n)
-            z_arrival(j, t).wait_recv()
             got = zgot[j, t]
-            return a + tab_z[0, t] * got, b + tab_z[1, t] * got
-
-        zero = jnp.zeros((HALF, HD), F32)
-        start = lax.fori_loop(1, Z, add_plane, (zero, zero))
+            start = (start[0] + tab_z[0, t] * got, start[1] + tab_z[1, t] * got)
 
         def step(p, carry):
             a, b = carry
@@ -321,21 +334,24 @@
         lax.fori_loop(0, XY, step, start)
         entering[(j // 2) * XY + me, j % 2] = ready[j, me]
 
-        def send(i, carry):
+        for i in range(1, XY):
             send_entering(j, i).start()
-            return carry
-
-        lax.fori_loop(1, XY, send, 0)
 
     def finish(j):
+        last = j == CHUNKS - 1
+        all_entering(2 * j).wait_recv()
+        if not last:
+            all_entering(2 * j + 1).wait_recv()
+
         def step(i, carry):
             p = behind(i)
             h = j * XY + p
 
-            @pl.when(i > 0)
-            def _():
-                entering_arrival(2 * j, i).wait_recv()
-                entering_arrival(2 * j + 1, i).wait_recv()
+            if last:
+
+                @pl.when(i > 0)
+                def _():
+                    last_entering(p).wait_recv()
 
             a = entering[h, :, 0].reshape(HD, HD)
             b = entering[h, :, 1].reshape(HD, HD)
@@ -348,9 +364,9 @@
             return carry
 
         lax.fori_loop(0, XY, step, 0)
-        for a in range(3):
-            for core in range(2):
-                swapped[a, j, core] = jnp.swapaxes(outs[a, pl.ds(j * XY, XY), core], 0, 1)
+
+    def swap_out(j, a, core):
+        swapped[a, j, core] = jnp.swapaxes(outs[a, pl.ds(j * XY, XY), core], 0, 1)
 
     def out_own(j, a):
         return pltpu.make_async_copy(
@@ -383,6 +399,10 @@
         for a in range(4):
             own_copy(j, a).wait()
         swap_in(j, c)
+    pl.semaphore_wait(barrier, XY + Z - 1)
+    for j in range(CHUNKS):
+        for a in range(4):
+            core_copy(j, a).start()
     for j in range(CHUNKS):
         for a in range(4):
             core_arrival(j, a).wait_recv()
@@ -404,28 +424,23 @@
     make_entering(PARTS - 2)
     make_entering(PARTS - 1)
     for j in range(CHUNKS):
+        for a in range(4):
+            core_copy(j, a).wait_send()
+    for u in range(PARTS):
+        all_sums(u).wait_send()
+        all_z(u).wait_send()
+    for j in range(CHUNKS):
         finish(j)
         for a in range(3):
+            swap_out(j, a, other)
+            out_core(j, a).start()
+        for a in range(3):
+            swap_out(j, a, c)
             out_own(j, a).start()
-            out_core(j, a).start()
 
     for u in range(PARTS):
-
-        def drain(i, carry):
-            send_sum(u, i).wait_send()
-            send_entering(u, i).wait_send()
-            return carry
-
-        lax.fori_loop(1, XY, drain, 0)
-
-        def drain_z(n, carry):
-            z_copy(u, n).wait_send()
-            return carry
-
-        lax.fori_loop(1, Z, drain_z, 0)
-    for j in range(CHUNKS):
-        for a in range(4):
-            core_copy(j, a).wait_send()
+        all_entering(u).wait_send()
+    for j in range(CHUNKS):
         for a in range(3):
             out_own(j, a).wait()
             out_core(j, a).wait_send()
@@ -466,12 +481,13 @@
             dma((CHUNKS, 4)),
             dma((CHUNKS, 4)),
             dma((CHUNKS, 4)),
-            dma((PARTS, XY)),
-            dma((PARTS, XY)),
-            dma((PARTS, Z)),
-            dma((PARTS, Z)),
-            dma((PARTS, XY)),
-            dma((PARTS, XY)),
+            dma((PARTS,)),
+            dma((PARTS,)),
+            dma((PARTS,)),
+            dma((PARTS,)),
+            dma((PARTS,)),
+            dma((PARTS - 1,)),
+            dma((XY,)),
             dma((CHUNKS, 3)),
             dma((CHUNKS, 3)),
             dma((CHUNKS, 3)),
@@ -482,13 +498,33 @@
     )(lengths, q, k, v, g)
 
 
+def store_kernel(a_ref, b_ref, c_ref, oa_ref, ob_ref, oc_ref, sems):
+    pairs = ((a_ref, oa_ref), (b_ref, ob_ref), (c_ref, oc_ref))
+    copies = [pltpu.make_async_copy(i, o, sems.at[n]) for n, (i, o) in enumerate(pairs)]
+    for copy in copies:
+        copy.start()
+    for copy in copies:
+        copy.wait()
+
+
+def store(results):
+    shape = jax.ShapeDtypeStruct(results[0].shape, BF16)
+    return pl.pallas_call(
+        store_kernel,
+        out_shape=(shape,) * 3,
+        in_specs=[pl.BlockSpec(memory_space=pltpu.VMEM)] * 3,
+        out_specs=(pl.BlockSpec(memory_space=pl.ANY),) * 3,
+        scratch_shapes=[pltpu.SemaphoreType.DMA((3,))],
+    )(*results)
+
+
 def build(mesh, Z, Y, X):
     def local(queries, key_heads, value_heads, grad_output, doc_lengths):
         tokens, heads, width = queries.shape
         all_tokens = tokens * Z * Y * X * 2
         scaling = 1.0 / math.sqrt(width * (all_tokens // 2))
         dims = (Z, Y, X, heads // 2, tokens)
-        return exchange(dims, scaling, doc_lengths, queries, key_heads, value_heads, grad_output)
+        return store(exchange(dims, scaling, doc_lengths, queries, key_heads, value_heads, grad_output))
 
     placed = P(("seq", "head"), None, None)
     return jax.shard_map(

time: 77.4 us -> 73.1 us (0.944)
  local copies, waits for them, and re-layouts: 4.93 us -> 0 us
    unnamed x7 -> x0, local copies, waits for them, and re-layouts: 4.93 us -> none
    pallas_call x0 -> x1, Pallas kernels: none -> 3.54 us  [store(): pl.pallas_call(store_kernel, out_shape=(shape,) * 3, in_specs=[pl.BlockSp...]
    pallas_call x1, Pallas kernels: 71.6 us -> 68.8 us  [exchange(): pl.pallas_call(functools.partial(kernel, dims, scaling), out_shape=(shape...]
where the time goes in v3:
time: 73.1 us; the launch traced here: 73 us
  Pallas kernels  72.3 us (99%)
    pallas_call x1, Pallas kernels, exchange(): pl.pallas_call(functools.partial(kernel, dims, scaling), out_shape=(shape...  68.8 us
    pallas_call x1, Pallas kernels, store(): pl.pallas_call(store_kernel, out_shape=(shape,) * 3, in_specs=[pl.BlockSp...  3.54 us

profile of v3, /device:TPU:1, one launch (start us, length us, event | category | flops | bytes accessed | tf_op | source)
XLA Modules:
  0.0 73.0 jit_solution(12371833812330648141)
XLA Ops:
  0.6 68.8 %shard_map.76 = (bf16[64,64,128]{2,1,0:T(8,128)(2,1)}, bf16[64,64,128]{2,1,0:T(8,128)(2,1)}, bf16[64,64,128]{2,1,0:T(8,128)(2,1)}) custom-call(s32[16]{0:T(128)} %len_ref.1, bf16[64,64,128]{2,1,0:T(8,128)(2,1)} %q_ref.1, bf16[64,64,128]{2,1,0:T(8,128)(2,1)} %k_ref.1, bf16[64,64,128]{2,1,0:T(8,128)(2,1)} %v_ref.1, bf16[64,64,128]{2,1,0:T(8,128)(2,1)} %g_ref.1), custom_call_target="tpu_custom_call" | custom-call | tf_op jit(solution)/shard_map/pallas_call | solution.py:459
  69.4 3.5 %shard_map.77 = (bf16[64,64,128]{2,1,0:T(8,128)(2,1)}, bf16[64,64,128]{2,1,0:T(8,128)(2,1)}, bf16[64,64,128]{2,1,0:T(8,128)(2,1)}) custom-call(bf16[64,64,128]{2,1,0:T(8,128)(2,1)} %get-tuple-element.6.a_ref, bf16[64,64,128]{2,1,0:T(8,128)(2,1)} %get-tuple-element.7.b_ref, bf16[64,64,128]{2,1,0:T(8,128)(2,1)} %get-tuple-element.8.c_ref), custom_call_target="tpu_custom_call" | custom-call | tf_op jit(solution)/shard_map/pallas_call | solution.py:512

commit v4 on v3

--- a/solution.py
+++ b/solution.py
@@ -16,8 +16,8 @@
 
 
 STEPS = (
-    (0, 0), (2, 2), (3, 2), (2, 3), (1, 2), (2, 1), (0, 2), (2, 0),
-    (3, 1), (1, 3), (3, 3), (1, 1), (0, 3), (3, 0), (0, 1), (1, 0),
+    (0, 0), (2, 2), (0, 2), (2, 1), (0, 3), (1, 2), (3, 2), (2, 3),
+    (3, 3), (1, 3), (3, 1), (2, 0), (1, 1), (3, 0), (0, 1), (1, 0),
 )
 STEPS_X = sum(dx << (2 * i) for i, (dx, dy) in enumerate(STEPS))
 STEPS_Y = sum(dy << (2 * i) for i, (dx, dy) in enumerate(STEPS))
@@ -29,11 +29,11 @@
 
 def kernel(
     dims, scaling,
-    len_ref, q_ref, k_ref, v_ref, g_ref,
+    len_hbm, q_ref, k_ref, v_ref, g_ref,
     oq_ref, ok_ref, ov_ref,
     raw, toks, sums, arrived, totals, zgot, ready, entering, part, outs, swapped, mask_f, mask_b,
-    ends, tab_p, tab_z,
-    own_sem, xs_sem, xr_sem, is_sem, ir_sem, zs_sem, zr_sem, os_sem, or_sem, last_sem, ys_sem, yr_sem, yl_sem,
+    len_ref, ends, tab_p, tab_z,
+    len_sem, own_sem, xs_sem, xr_sem, is_sem, ir_sem, zs_sem, zr_sem, os_sem, or_sem, last_sem, ys_sem, yr_sem, yl_sem,
 ):
     Z, Y, X, NH, TK = dims
     XY = X * Y
@@ -75,6 +75,8 @@
     def z_step(n):
         return (z + (((n + 1) // 2) if n % 2 else Z - n // 2)) % Z
 
+    lengths = pltpu.make_async_copy(len_hbm, len_ref, len_sem)
+    lengths.start()
     barrier = pltpu.get_barrier_semaphore()
 
     def greet(device):
@@ -119,6 +121,7 @@
         for a in range(4):
             own_copy(j, a).start()
 
+    lengths.wait()
     total_len = jnp.int32(0)
     for d in range(NDOC):
         total_len = total_len + len_ref[d]
@@ -459,7 +462,7 @@
     return pl.pallas_call(
         functools.partial(kernel, dims, scaling),
         out_shape=(shape, shape, shape),
-        in_specs=[pl.BlockSpec(memory_space=pltpu.SMEM)] + [pl.BlockSpec(memory_space=pl.ANY)] * 4,
+        in_specs=[pl.BlockSpec(memory_space=pl.ANY)] * 5,
         out_specs=(pl.BlockSpec(memory_space=pl.ANY),) * 3,
         scratch_shapes=[
             pltpu.VMEM((4, CHUNKS, 2, TK, XY, HD), BF16),
@@ -476,8 +479,10 @@
             pltpu.VMEM((3, CT, HD), F32),
             pltpu.VMEM((2, CT, HD), BF16),
             pltpu.SMEM((NDOC,), jnp.int32),
+            pltpu.SMEM((NDOC,), jnp.int32),
             pltpu.SMEM((4, XY), F32),
             pltpu.SMEM((2, Z), F32),
+            dma,
             dma((CHUNKS, 4)),
             dma((CHUNKS, 4)),
             dma((CHUNKS, 4)),
@@ -498,13 +503,24 @@
     )(lengths, q, k, v, g)
 
 
-def store_kernel(a_ref, b_ref, c_ref, oa_ref, ob_ref, oc_ref, sems):
-    pairs = ((a_ref, oa_ref), (b_ref, ob_ref), (c_ref, oc_ref))
-    copies = [pltpu.make_async_copy(i, o, sems.at[n]) for n, (i, o) in enumerate(pairs)]
-    for copy in copies:
-        copy.start()
-    for copy in copies:
-        copy.wait()
+PIECES = 4
+
+
+def store_kernel(a_ref, b_ref, c_ref, oa_ref, ob_ref, oc_ref, held, in_sems, out_sems):
+    size = a_ref.shape[0] // PIECES
+    loads, stores = [], []
+    for n, (source, target) in enumerate(((a_ref, oa_ref), (b_ref, ob_ref), (c_ref, oc_ref))):
+        for m in range(PIECES):
+            rows = pl.ds(m * size, size)
+            loads.append(pltpu.make_async_copy(source.at[rows], held.at[n, rows], in_sems.at[n, m]))
+            stores.append(pltpu.make_async_copy(held.at[n, rows], target.at[rows], out_sems.at[n, m]))
+    for load in loads:
+        load.start()
+    for load, store_piece in zip(loads, stores):
+        load.wait()
+        store_piece.start()
+    for store_piece in stores:
+        store_piece.wait()
 
 
 def store(results):
@@ -512,9 +528,13 @@
     return pl.pallas_call(
         store_kernel,
         out_shape=(shape,) * 3,
-        in_specs=[pl.BlockSpec(memory_space=pltpu.VMEM)] * 3,
+        in_specs=[pl.BlockSpec(memory_space=pl.ANY)] * 3,
         out_specs=(pl.BlockSpec(memory_space=pl.ANY),) * 3,
-        scratch_shapes=[pltpu.SemaphoreType.DMA((3,))],
+        scratch_shapes=[
+            pltpu.VMEM((3,) + results[0].shape, BF16),
+            pltpu.SemaphoreType.DMA((3, PIECES)),
+            pltpu.SemaphoreType.DMA((3, PIECES)),
+        ],
     )(*results)
 
 

time: 73.1 us -> 70.2 us (0.960)
  Pallas kernels: 72.3 us -> 69.4 us
    pallas_call x1, Pallas kernels: 68.8 us -> 66.6 us  [exchange(): pl.pallas_call(functools.partial(kernel, dims, scaling), out_shape=(shape...]
    pallas_call x1, Pallas kernels: 3.54 us -> 2.81 us  [store(): pl.pallas_call(store_kernel, out_shape=(shape,) * 3, in_specs=[pl.BlockSp...]
where the time goes in v4:
time: 70.2 us; the launch traced here: 70.1 us
  Pallas kernels  69.4 us (99%)
    pallas_call x1, Pallas kernels, exchange(): pl.pallas_call(functools.partial(kernel, dims, scaling), out_shape=(shape...  66.6 us
    pallas_call x1, Pallas kernels, store(): pl.pallas_call(store_kernel, out_shape=(shape,) * 3, in_specs=[pl.BlockSp...  2.81 us

profile of v4, /device:TPU:1, one launch (start us, length us, event | category | flops | bytes accessed | tf_op | source)
XLA Modules:
  0.0 70.1 jit_solution(3038375214558586311)
XLA Ops:
  0.6 66.6 %shard_map.76 = (bf16[64,64,128]{2,1,0:T(8,128)(2,1)}, bf16[64,64,128]{2,1,0:T(8,128)(2,1)}, bf16[64,64,128]{2,1,0:T(8,128)(2,1)}) custom-call(s32[16]{0:T(128)} %len_hbm.1, bf16[64,64,128]{2,1,0:T(8,128)(2,1)} %q_ref.1, bf16[64,64,128]{2,1,0:T(8,128)(2,1)} %k_ref.1, bf16[64,64,128]{2,1,0:T(8,128)(2,1)} %v_ref.1, bf16[64,64,128]{2,1,0:T(8,128)(2,1)} %g_ref.1), custom_call_target="tpu_custom_call" | custom-call | tf_op jit(solution)/shard_map/pallas_call | solution.py:462
  67.3 2.8 %shard_map.77 = (bf16[64,64,128]{2,1,0:T(8,128)(2,1)}, bf16[64,64,128]{2,1,0:T(8,128)(2,1)}, bf16[64,64,128]{2,1,0:T(8,128)(2,1)}) custom-call(bf16[64,64,128]{2,1,0:T(8,128)(2,1)} %get-tuple-element.6.a_ref, bf16[64,64,128]{2,1,0:T(8,128)(2,1)} %get-tuple-element.7.b_ref, bf16[64,64,128]{2,1,0:T(8,128)(2,1)} %get-tuple-element.8.c_ref), custom_call_target="tpu_custom_call" | custom-call | tf_op jit(solution)/shard_map/pallas_call | solution.py:528

commit v5 on v3

--- a/solution.py
+++ b/solution.py
@@ -16,8 +16,8 @@
 
 
 STEPS = (
-    (0, 0), (2, 2), (3, 2), (2, 3), (1, 2), (2, 1), (0, 2), (2, 0),
-    (3, 1), (1, 3), (3, 3), (1, 1), (0, 3), (3, 0), (0, 1), (1, 0),
+    (0, 0), (2, 2), (0, 2), (2, 1), (0, 3), (1, 2), (3, 2), (2, 3),
+    (3, 3), (1, 3), (3, 1), (2, 0), (1, 1), (3, 0), (0, 1), (1, 0),
 )
 STEPS_X = sum(dx << (2 * i) for i, (dx, dy) in enumerate(STEPS))
 STEPS_Y = sum(dy << (2 * i) for i, (dx, dy) in enumerate(STEPS))
@@ -29,11 +29,11 @@
 
 def kernel(
     dims, scaling,
-    len_ref, q_ref, k_ref, v_ref, g_ref,
+    len_hbm, q_ref, k_ref, v_ref, g_ref,
     oq_ref, ok_ref, ov_ref,
     raw, toks, sums, arrived, totals, zgot, ready, entering, part, outs, swapped, mask_f, mask_b,
-    ends, tab_p, tab_z,
-    own_sem, xs_sem, xr_sem, is_sem, ir_sem, zs_sem, zr_sem, os_sem, or_sem, last_sem, ys_sem, yr_sem, yl_sem,
+    len_ref, ends, tab_p, tab_z,
+    len_sem, own_sem, xs_sem, xr_sem, is_sem, ir_sem, zs_sem, zr_sem, os_sem, or_sem, last_sem, ys_sem, yr_sem, yl_sem,
 ):
     Z, Y, X, NH, TK = dims
     XY = X * Y
@@ -75,6 +75,8 @@
     def z_step(n):
         return (z + (((n + 1) // 2) if n % 2 else Z - n // 2)) % Z
 
+    lengths = pltpu.make_async_copy(len_hbm, len_ref, len_sem)
+    lengths.start()
     barrier = pltpu.get_barrier_semaphore()
 
     def greet(device):
@@ -119,6 +121,7 @@
         for a in range(4):
             own_copy(j, a).start()
 
+    lengths.wait()
     total_len = jnp.int32(0)
     for d in range(NDOC):
         total_len = total_len + len_ref[d]
@@ -220,7 +223,7 @@
 
             return carry
 
-        lax.fori_loop(1, XY + 1, step, 0)
+        lax.fori_loop(1, XY + 1, step, 0, unroll=2)
 
         for i in range(1, XY):
             send_sum(2 * j + 1, i).start()
@@ -270,7 +273,7 @@
             return a, b
 
         zero = jnp.zeros((HALF, HD), F32)
-        a, b = lax.fori_loop(0, XY, step, (zero, zero))
+        a, b = lax.fori_loop(0, XY, step, (zero, zero), unroll=4)
         totals[j, 0] = a
         totals[j, 1] = b
 
@@ -331,7 +334,7 @@
             b = tab_p[2, r] * b + arrived[j, r, 1].astype(F32)
             return a, b
 
-        lax.fori_loop(0, XY, step, start)
+        lax.fori_loop(0, XY, step, start, unroll=4)
         entering[(j // 2) * XY + me, j % 2] = ready[j, me]
 
         for i in range(1, XY):
@@ -363,7 +366,7 @@
             outs[2, h] = dv.astype(BF16).reshape(2, TK, HD)
             return carry
 
-        lax.fori_loop(0, XY, step, 0)
+        lax.fori_loop(0, XY, step, 0, unroll=2)
 
     def swap_out(j, a, core):
         swapped[a, j, core] = jnp.swapaxes(outs[a, pl.ds(j * XY, XY), core], 0, 1)
@@ -459,7 +462,7 @@
     return pl.pallas_call(
         functools.partial(kernel, dims, scaling),
         out_shape=(shape, shape, shape),
-        in_specs=[pl.BlockSpec(memory_space=pltpu.SMEM)] + [pl.BlockSpec(memory_space=pl.ANY)] * 4,
+        in_specs=[pl.BlockSpec(memory_space=pl.ANY)] * 5,
         out_specs=(pl.BlockSpec(memory_space=pl.ANY),) * 3,
         scratch_shapes=[
             pltpu.VMEM((4, CHUNKS, 2, TK, XY, HD), BF16),
@@ -476,8 +479,10 @@
             pltpu.VMEM((3, CT, HD), F32),
             pltpu.VMEM((2, CT, HD), BF16),
             pltpu.SMEM((NDOC,), jnp.int32),
+            pltpu.SMEM((NDOC,), jnp.int32),
             pltpu.SMEM((4, XY), F32),
             pltpu.SMEM((2, Z), F32),
+            dma,
             dma((CHUNKS, 4)),
             dma((CHUNKS, 4)),
             dma((CHUNKS, 4)),
@@ -493,7 +498,7 @@
             dma((CHUNKS, 3)),
         ],
         compiler_params=pltpu.CompilerParams(
-            collective_id=0, has_side_effects=True, vmem_limit_bytes=56 << 20
+            collective_id=0, has_side_effects=True, vmem_limit_bytes=50 << 20
         ),
     )(lengths, q, k, v, g)
 
@@ -513,8 +518,9 @@
         store_kernel,
         out_shape=(shape,) * 3,
         in_specs=[pl.BlockSpec(memory_space=pltpu.VMEM)] * 3,
-        out_specs=(pl.BlockSpec(memory_space=pl.ANY),) * 3,
+        out_specs=(pl.BlockSpec(memory_space=pltpu.HBM),) * 3,
         scratch_shapes=[pltpu.SemaphoreType.DMA((3,))],
+        compiler_params=pltpu.CompilerParams(vmem_limit_bytes=8 << 20),
     )(*results)
 
 

time: 73.1 us -> 69.9 us (0.956)
  Pallas kernels: 72.3 us -> 68.5 us
    pallas_call x1, Pallas kernels: 68.8 us -> 66.8 us  [exchange(): pl.pallas_call(functools.partial(kernel, dims, scaling), out_shape=(shape...]
    pallas_call x1, Pallas kernels: 3.54 us -> 1.69 us  [store(): pl.pallas_call(store_kernel, out_shape=(shape,) * 3, in_specs=[pl.BlockSp...]
where the time goes in v5:
time: 69.9 us; the launch traced here: 69.8 us
  Pallas kernels  68.5 us (98%)
    pallas_call x1, Pallas kernels, exchange(): pl.pallas_call(functools.partial(kernel, dims, scaling), out_shape=(shape...  66.8 us
    pallas_call x1, Pallas kernels, store(): pl.pallas_call(store_kernel, out_shape=(shape,) * 3, in_specs=[pl.BlockSp...  1.69 us

profile of v5, /device:TPU:1, one launch (start us, length us, event | category | flops | bytes accessed | tf_op | source)
XLA Modules:
  0.0 69.8 jit_solution(2306658588590093605)
XLA Ops:
  0.6 0.0 copy-start
  0.6 0.6 copy-done
  1.3 66.8 %shard_map.76 = (bf16[64,64,128]{2,1,0:T(8,128)(2,1)S(1)}, bf16[64,64,128]{2,1,0:T(8,128)(2,1)S(1)}, bf16[64,64,128]{2,1,0:T(8,128)(2,1)S(1)}) custom-call(s32[16]{0:T(128)S(1)} %copy-done, bf16[64,64,128]{2,1,0:T(8,128)(2,1)} %q_ref.1, bf16[64,64,128]{2,1,0:T(8,128)(2,1)} %k_ref.1, bf16[64,64,128]{2,1,0:T(8,128)(2,1)} %v_ref.1, bf16[64,64,128]{2,1,0:T(8,128)(2,1)} %g_ref.1), custom_call_target="tpu_custom_call" | custom-call | tf_op jit(solution)/shard_map/pallas_call | solution.py:462
  68.1 1.7 %shard_map.77 = (bf16[64,64,128]{2,1,0:T(8,128)(2,1)}, bf16[64,64,128]{2,1,0:T(8,128)(2,1)}, bf16[64,64,128]{2,1,0:T(8,128)(2,1)}) custom-call(bf16[64,64,128]{2,1,0:T(8,128)(2,1)S(1)} %get-tuple-element.6.a_ref, bf16[64,64,128]{2,1,0:T(8,128)(2,1)S(1)} %get-tuple-element.7.b_ref, bf16[64,64,128]{2,1,0:T(8,128)(2,1)S(1)} %get-tuple-element.8.c_ref), custom_call_target="tpu_custom_call" | custom-call | tf_op jit(solution)/shard_map/pallas_call | solution.py:517
Async XLA Ops:
  0.6 0.7 copy-start

commit v6 on v5

--- a/solution.py
+++ b/solution.py
@@ -421,8 +421,10 @@
     piece = NH // PARTS
     for u in range(PARTS):
         local_work(u * piece, (u + 1) * piece)
+        if u == PARTS - 1:
+            make_entering(u - 2)
         gather(u)
-        if u >= 2:
+        if 2 <= u < PARTS - 1:
             make_entering(u - 2)
     make_entering(PARTS - 2)
     make_entering(PARTS - 1)

time: 69.9 us -> 69.9 us (level)
  no operation moved by 1% of the time
where the time goes in v6:
time: 69.9 us; the launch traced here: 69.8 us
  Pallas kernels  68.5 us (98%)
    pallas_call x1, Pallas kernels, exchange(): pl.pallas_call(functools.partial(kernel, dims, scaling), out_shape=(shape...  66.8 us
    pallas_call x1, Pallas kernels, store(): pl.pallas_call(store_kernel, out_shape=(shape,) * 3, in_specs=[pl.BlockSp...  1.69 us

profile of v6, /device:TPU:1, one launch (start us, length us, event | category | flops | bytes accessed | tf_op | source)
XLA Modules:
  0.0 69.8 jit_solution(5790633324421214308)
XLA Ops:
  0.6 0.0 copy-start
  0.6 0.6 copy-done
  1.3 66.8 %shard_map.76 = (bf16[64,64,128]{2,1,0:T(8,128)(2,1)S(1)}, bf16[64,64,128]{2,1,0:T(8,128)(2,1)S(1)}, bf16[64,64,128]{2,1,0:T(8,128)(2,1)S(1)}) custom-call(s32[16]{0:T(128)S(1)} %copy-done, bf16[64,64,128]{2,1,0:T(8,128)(2,1)} %q_ref.1, bf16[64,64,128]{2,1,0:T(8,128)(2,1)} %k_ref.1, bf16[64,64,128]{2,1,0:T(8,128)(2,1)} %v_ref.1, bf16[64,64,128]{2,1,0:T(8,128)(2,1)} %g_ref.1), custom_call_target="tpu_custom_call" | custom-call | tf_op jit(solution)/shard_map/pallas_call | solution.py:464
  68.1 1.7 %shard_map.77 = (bf16[64,64,128]{2,1,0:T(8,128)(2,1)}, bf16[64,64,128]{2,1,0:T(8,128)(2,1)}, bf16[64,64,128]{2,1,0:T(8,128)(2,1)}) custom-call(bf16[64,64,128]{2,1,0:T(8,128)(2,1)S(1)} %get-tuple-element.6.a_ref, bf16[64,64,128]{2,1,0:T(8,128)(2,1)S(1)} %get-tuple-element.7.b_ref, bf16[64,64,128]{2,1,0:T(8,128)(2,1)S(1)} %get-tuple-element.8.c_ref), custom_call_target="tpu_custom_call" | custom-call | tf_op jit(solution)/shard_map/pallas_call | solution.py:519
Async XLA Ops:
  0.6 0.7 copy-start
